TPU v7x, 32 devices: a whole 2x2x4 slice. The times are simulated.
32 devices in a mesh: wide: 16 (over z, x, core), narrow: 2 (over y).
Axes of the slice: x: 2, y: 2, z: 4, core: 2. Of those that a mesh axis runs over, the one named last changes fastest.
Arguments:
- tokens: bfloat16 [16384, 512], P(('wide', 'narrow')), may hold values from -6 to 6
- input_weight: bfloat16 [2, 512, 3, 512], P(None, None, None, 'narrow'), may hold values from -0.25 to 0.25
- query_bias: float32 [2, 512], P(None, 'narrow'), may hold values from -4 to 4
- value_bias: float32 [2, 512], P(None, 'narrow'), may hold values from -0.5 to 0.5
- output_weight: bfloat16 [2, 512, 512], P(None, 'narrow'), may hold values from -4 to 4
- output_bias: float32 [2, 512], replicated, may hold values from -3 to 3
- first_gain: float32 [2, 512], replicated, may hold values from 0.5 to 1.5
- first_shift: float32 [2, 512], replicated, may hold values from -3 to 3
- expand_weight: bfloat16 [2, 512, 2048], P(None, None, 'narrow'), may hold values from -0.25 to 0.25
- expand_bias: float32 [2, 2048], P(None, 'narrow'), may hold values from -3 to 3
- shrink_weight: bfloat16 [2, 2048, 512], P(None, 'narrow'), may hold values from -0.125 to 0.125
- shrink_bias: float32 [2, 512], replicated, may hold values from -3 to 3
- second_gain: float32 [2, 512], replicated, may hold values from 0.5 to 1.5
- second_shift: float32 [2, 512], replicated, may hold values from -3 to 3
- lengths: int32 [32], P('wide'), may hold values from 0 to 1024, as said below
- bucket: int32 [16], P('wide'), may hold values from 0 to 1, as said below
- cotangent: bfloat16 [16384, 512], P(('wide', 'narrow')), may hold values from -6 to 6
Outputs:
- layer_output: float32 [16384, 512], P(('wide', 'narrow'))
- input_grad: float32 [16384, 512], P(('wide', 'narrow'))
- input_weight_grad: float32 [2, 512, 3, 512], P(None, None, None, 'narrow')
- query_bias_grad: float32 [2, 512], P(None, 'narrow')
- value_bias_grad: float32 [2, 512], P(None, 'narrow')
- output_weight_grad: float32 [2, 512, 512], P(None, 'narrow')
- output_bias_grad: float32 [2, 512], replicated
- first_gain_grad: float32 [2, 512], replicated
- first_shift_grad: float32 [2, 512], replicated
- expand_weight_grad: float32 [2, 512, 2048], P(None, None, 'narrow')
- expand_bias_grad: float32 [2, 2048], P(None, 'narrow')
- shrink_weight_grad: float32 [2, 2048, 512], P(None, 'narrow')
- shrink_bias_grad: float32 [2, 512], replicated
- second_gain_grad: float32 [2, 512], replicated
- second_shift_grad: float32 [2, 512], replicated
Inputs may be any that keep to these rules, and one draw needn't show every extreme that they name: Entries 2 i and 2 i + 1 are the lengths of the sequences of index i of wide: either 1024 and 0 or half of 1024 twice; exactly half of the indices hold a single sequence. `bucket`: 0 where index i of wide holds one sequence of 1024 tokens, 1 where it holds two of half that length; agrees with lengths.
All inputs are finite; a program needn't handle non-finite values.
Results may differ from a plain program's by a relative error of at most 0.025.
Values may be sent and summed in bfloat16 or wider, within the bound.
A program may use at most 128 MiB of HBM per device.

v0:
```python
import jax
import jax.numpy as jnp
from jax import lax
from jax.sharding import PartitionSpec as P

DH = 64


EPSILON = 1e-12
MASKED = -1000000000.0


def layer_norm(values, gain, shift):
    centre = values - jnp.mean(values, -1, keepdims=True)
    spread = jnp.mean(centre * centre, -1, keepdims=True)
    return centre * lax.rsqrt(spread + EPSILON) * gain + shift


def gelu_exact(values):
    return jax.nn.gelu(values, approximate=False)


def masked_scores(query_rows, query_seg, key_rows, segment, scaling):
    scores = (
        jnp.einsum("qhd,khd->hqk", query_rows, key_rows, preferred_element_type=jnp.float32)
        * scaling
    )
    return jnp.where((query_seg[:, None] == segment[None, :])[None], scores, MASKED)


def attend_forward(queries, key_rows, value_rows, segment, scaling):
    total_rows = queries.shape[0]
    block_rows = min(total_rows, 512)
    block_count = total_rows // block_rows

    def one_block(inputs):
        query_rows, query_seg = inputs
        scores = masked_scores(query_rows, query_seg, key_rows, segment, scaling)
        row_peak = jnp.max(scores, -1, keepdims=True)
        weights = jnp.exp(scores - row_peak)
        totals = jnp.sum(weights, -1, keepdims=True)
        softmax_low = (weights / totals).astype(jnp.bfloat16)
        mixed_rows = jnp.einsum(
            "hqk,khd->qhd", softmax_low, value_rows, preferred_element_type=jnp.float32
        )
        return (mixed_rows, (row_peak + jnp.log(totals))[..., 0])

    mixed_rows, log_total = lax.map(
        one_block,
        (
            queries.reshape((block_count, block_rows) + queries.shape[1:]),
            segment.reshape(block_count, block_rows),
        ),
    )
    return (mixed_rows.reshape(queries.shape), log_total)


def attend_backward(queries, key_rows, value_rows, segment, log_total, mixed_grad, scaling):
    total_rows = queries.shape[0]
    block_rows = min(total_rows, 512)
    block_count = total_rows // block_rows
    block_shape = (block_count, block_rows) + queries.shape[1:]

    def one_block(carried, inputs):
        key_grad, value_grad = carried
        query_rows, query_seg, row_total, grad_rows = inputs
        scores = masked_scores(query_rows, query_seg, key_rows, segment, scaling)
        softmax_rows = jnp.exp(scores - row_total[..., None])
        value_grad = value_grad + jnp.einsum(
            "hqk,qhd->khd",
            softmax_rows.astype(jnp.bfloat16),
            grad_rows,
            preferred_element_type=jnp.float32,
        )
        softmax_grad = jnp.einsum(
            "qhd,khd->hqk", grad_rows, value_rows, preferred_element_type=jnp.float32
        )
        inner_sum = jnp.sum(softmax_rows * softmax_grad, -1, keepdims=True)
        score_grad = (softmax_rows * (softmax_grad - inner_sum)).astype(jnp.bfloat16)
        query_grad = (
            jnp.einsum("hqk,khd->qhd", score_grad, key_rows, preferred_element_type=jnp.float32)
            * scaling
        )
        key_grad = (
            key_grad
            + jnp.einsum("hqk,qhd->khd", score_grad, query_rows, preferred_element_type=jnp.float32)
            * scaling
        )
        return ((key_grad, value_grad), query_grad)

    zero_grads = jnp.zeros(queries.shape, jnp.float32)
    (key_grad, value_grad), query_grad = lax.scan(
        one_block,
        (zero_grads, zero_grads),
        (
            queries.reshape(block_shape),
            segment.reshape(block_count, block_rows),
            log_total,
            mixed_grad.reshape(block_shape),
        ),
    )
    return (query_grad.reshape(queries.shape), key_grad, value_grad)


def forward_layer(hidden, weights_all, segment, scaling):
    (
        input_weight,
        query_bias,
        value_bias,
        output_weight,
        output_bias,
        first_gain,
        first_shift,
        expand_weight,
        expand_bias,
        shrink_weight,
        shrink_bias,
        second_gain,
        second_shift,
    ) = weights_all
    hidden_low = lax.all_gather(hidden.astype(jnp.bfloat16), "narrow", axis=0, tiled=True)
    total_rows = hidden_low.shape[0]
    head_shape = (total_rows, query_bias.shape[0] // DH, DH)
    triple = jnp.einsum("td,dce->tce", hidden_low, input_weight, preferred_element_type=jnp.float32)
    queries = (triple[:, 0] + query_bias).astype(jnp.bfloat16).reshape(head_shape)
    key_rows = triple[:, 1].astype(jnp.bfloat16).reshape(head_shape)
    value_rows = (triple[:, 2] + value_bias).astype(jnp.bfloat16).reshape(head_shape)
    mixed_rows, log_total = attend_forward(queries, key_rows, value_rows, segment, scaling)
    mixed_low = mixed_rows.reshape(total_rows, -1).astype(jnp.bfloat16)
    summed = (
        hidden
        + lax.psum_scatter(
            jnp.dot(mixed_low, output_weight, preferred_element_type=jnp.float32).astype(
                jnp.bfloat16
            ),
            "narrow",
            scatter_dimension=0,
            tiled=True,
        ).astype(jnp.float32)
        + output_bias
    )
    normed = layer_norm(summed, first_gain, first_shift)
    normed_low = lax.all_gather(normed.astype(jnp.bfloat16), "narrow", axis=0, tiled=True)
    inner_rows = (
        jnp.dot(normed_low, expand_weight, preferred_element_type=jnp.float32) + expand_bias
    )
    activated = gelu_exact(inner_rows).astype(jnp.bfloat16)
    widened = (
        normed
        + lax.psum_scatter(
            jnp.dot(activated, shrink_weight, preferred_element_type=jnp.float32).astype(
                jnp.bfloat16
            ),
            "narrow",
            scatter_dimension=0,
            tiled=True,
        ).astype(jnp.float32)
        + shrink_bias
    )
    kept = (
        hidden_low,
        queries,
        key_rows,
        value_rows,
        log_total,
        mixed_low,
        summed,
        normed_low,
        inner_rows,
        activated,
        widened,
    )
    return (layer_norm(widened, second_gain, second_shift), kept)


def backward_layer(grad_rows, weights_all, kept, segment, scaling):
    (
        input_weight,
        query_bias,
        value_bias,
        output_weight,
        output_bias,
        first_gain,
        first_shift,
        expand_weight,
        expand_bias,
        shrink_weight,
        shrink_bias,
        second_gain,
        second_shift,
    ) = weights_all
    (
        hidden_low,
        queries,
        key_rows,
        value_rows,
        log_total,
        mixed_low,
        summed,
        normed_low,
        inner_rows,
        activated,
        widened,
    ) = kept
    total_rows = hidden_low.shape[0]
    unused, second_pull = jax.vjp(layer_norm, widened, second_gain, second_shift)
    widened_grad, second_gain_grad, second_shift_grad = second_pull(grad_rows)
    shrink_bias_grad = jnp.sum(widened_grad, 0)
    branch_low = lax.all_gather(widened_grad.astype(jnp.bfloat16), "narrow", axis=0, tiled=True)
    shrink_weight_grad = jnp.einsum(
        "tf,td->fd", activated, branch_low, preferred_element_type=jnp.float32
    )
    activated_grad = jnp.einsum(
        "td,fd->tf", branch_low, shrink_weight, preferred_element_type=jnp.float32
    )
    unused, gelu_pull = jax.vjp(gelu_exact, inner_rows)
    inner_low = gelu_pull(activated_grad)[0].astype(jnp.bfloat16)
    expand_bias_grad = jnp.sum(inner_low, 0, dtype=jnp.float32)
    expand_weight_grad = jnp.einsum(
        "td,tf->df", normed_low, inner_low, preferred_element_type=jnp.float32
    )
    normed_grad = widened_grad + lax.psum_scatter(
        jnp.einsum(
            "tf,df->td", inner_low, expand_weight, preferred_element_type=jnp.float32
        ).astype(jnp.bfloat16),
        "narrow",
        scatter_dimension=0,
        tiled=True,
    ).astype(jnp.float32)
    unused, first_pull = jax.vjp(layer_norm, summed, first_gain, first_shift)
    summed_grad, first_gain_grad, first_shift_grad = first_pull(normed_grad)
    output_bias_grad = jnp.sum(summed_grad, 0)
    mix_low = lax.all_gather(summed_grad.astype(jnp.bfloat16), "narrow", axis=0, tiled=True)
    output_weight_grad = jnp.einsum(
        "te,td->ed", mixed_low, mix_low, preferred_element_type=jnp.float32
    )
    mixed_grad = (
        jnp.einsum("td,ed->te", mix_low, output_weight, preferred_element_type=jnp.float32)
        .astype(jnp.bfloat16)
        .reshape(queries.shape)
    )
    query_grad, key_grad, value_grad = attend_backward(
        queries, key_rows, value_rows, segment, log_total, mixed_grad, scaling
    )
    triple_grad = (
        jnp.stack([query_grad, key_grad, value_grad], 1)
        .reshape(total_rows, 3, -1)
        .astype(jnp.bfloat16)
    )
    query_bias_grad = jnp.sum(triple_grad[:, 0], 0, dtype=jnp.float32)
    value_bias_grad = jnp.sum(triple_grad[:, 2], 0, dtype=jnp.float32)
    input_weight_grad = jnp.einsum(
        "td,tce->dce", hidden_low, triple_grad, preferred_element_type=jnp.float32
    )
    hidden_grad = summed_grad + lax.psum_scatter(
        jnp.einsum(
            "tce,dce->td", triple_grad, input_weight, preferred_element_type=jnp.float32
        ).astype(jnp.bfloat16),
        "narrow",
        scatter_dimension=0,
        tiled=True,
    ).astype(jnp.float32)
    sharded = (
        input_weight_grad,
        query_bias_grad,
        value_bias_grad,
        output_weight_grad,
        expand_weight_grad,
        expand_bias_grad,
        shrink_weight_grad,
    )
    shared = (
        output_bias_grad,
        first_gain_grad,
        first_shift_grad,
        shrink_bias_grad,
        second_gain_grad,
        second_shift_grad,
    )
    return (hidden_grad, sharded, shared)


def local(
    tokens,
    input_weight,
    query_bias,
    value_bias,
    output_weight,
    output_bias,
    first_gain,
    first_shift,
    expand_weight,
    expand_bias,
    shrink_weight,
    shrink_bias,
    second_gain,
    second_shift,
    lengths,
    bucket,
    cotangent,
):
    total_rows = tokens.shape[0] * lax.axis_size("narrow")
    scaling = DH ** (-0.5)
    boundary = jnp.where(bucket[0] == 1, lengths[0], total_rows)
    segment = (jnp.arange(total_rows, dtype=jnp.int32) >= boundary).astype(jnp.int32)
    stacked = (
        input_weight,
        query_bias,
        value_bias,
        output_weight,
        output_bias,
        first_gain,
        first_shift,
        expand_weight,
        expand_bias,
        shrink_weight,
        shrink_bias,
        second_gain,
        second_shift,
    )
    layer_count = input_weight.shape[0]
    hidden = tokens.astype(jnp.float32)
    saved = []
    for layer_index in range(layer_count):
        hidden, kept = forward_layer(
            hidden, tuple((item[layer_index] for item in stacked)), segment, scaling
        )
        saved.append(kept)
    grad_rows = cotangent.astype(jnp.float32)
    sharded_list = []
    shared_list = []
    for layer_index in reversed(range(layer_count)):
        grad_rows, sharded, shared = backward_layer(
            grad_rows,
            tuple((item[layer_index] for item in stacked)),
            saved[layer_index],
            segment,
            scaling,
        )
        sharded_list.insert(0, sharded)
        shared_list.insert(0, shared)
    sharded_all = tuple(
        (jnp.stack([entry[position] for entry in sharded_list]) for position in range(7))
    )
    shared_all = tuple(
        (jnp.stack([entry[position] for entry in shared_list]) for position in range(6))
    )
    grad_input, grad_query, grad_value, grad_output, grad_expand, grad_expand_bias, grad_shrink = (
        sharded_all
    )
    (
        grad_output_bias,
        grad_first_gain,
        grad_first_shift,
        grad_shrink_bias,
        grad_second_gain,
        grad_second_shift,
    ) = shared_all
    sharded_all = lax.psum(
        (
            grad_input,
            grad_query,
            grad_value,
            grad_output,
            grad_expand,
            grad_expand_bias,
            grad_shrink,
        ),
        "wide",
    )
    shared_all = lax.psum(
        (
            grad_output_bias,
            grad_first_gain,
            grad_first_shift,
            grad_shrink_bias,
            grad_second_gain,
            grad_second_shift,
        ),
        ("wide", "narrow"),
    )
    return (
        hidden,
        grad_rows,
        sharded_all[0],
        sharded_all[1],
        sharded_all[2],
        sharded_all[3],
        shared_all[0],
        shared_all[1],
        shared_all[2],
        sharded_all[4],
        sharded_all[5],
        sharded_all[6],
        shared_all[3],
        shared_all[4],
        shared_all[5],
    )


def solution(mesh):
    in_specs = (
        P(("wide", "narrow"), None),
        P(None, None, None, "narrow"),
        P(None, "narrow"),
        P(None, "narrow"),
        P(None, "narrow", None),
        P(),
        P(),
        P(),
        P(None, None, "narrow"),
        P(None, "narrow"),
        P(None, "narrow", None),
        P(),
        P(),
        P(),
        P("wide"),
        P("wide"),
        P(("wide", "narrow"), None),
    )
    out_specs = (
        P(("wide", "narrow"), None),
        P(("wide", "narrow"), None),
        P(None, None, None, "narrow"),
        P(None, "narrow"),
        P(None, "narrow"),
        P(None, "narrow", None),
        P(),
        P(),
        P(),
        P(None, None, "narrow"),
        P(None, "narrow"),
        P(None, "narrow", None),
        P(),
        P(),
        P(),
    )
    return jax.shard_map(local, mesh=mesh, in_specs=in_specs, out_specs=out_specs, check_vma=False)
```

profile of v0, /device:TPU:0, one launch (start us, length us, event | category | flops | bytes accessed | tf_op | source)
XLA Modules:
  0.0 833.4 jit_solution(17096664330684650404)
XLA Ops:
  10.2 23.4 %all-gather.9.cloned.1.call-done = bf16[1024,512]{1,0:T(8,128)(2,1)} async-done(((bf16[512,512]{1,0:T(8,128)(2,1)}), bf16[1024,512]{1,0:T(8,128)(2,1)}) %all-gather.9.cloned.1.call-update) | async-done | bytes 1048592 | tf_op jit(solution)/shard_map/all_gather | solution.py:121
  40.5 16.1 %while.56 = (s32[]{:T(128)}, bf16[2,512,4,64]{1,3,2,0:T(8,128)(2,1)S(1)}, f32[2,4,512]{2,1,0:T(4,128)}, s32[2,512]{1,0:T(2,128)S(1)}, bf16[2,512,4,64]{1,3,2,0:T...) while((s32[]{:T(128)}, ...), condition=%wide.region_3.4_spmd.clone, body=%wide.region_0.3_spmd.clone.sunk | while | flops 562561024 | bytes 29177976 | solution.py:48
  59.7 20.4 %reduce-scatter.9.cloned.1.call-done = bf16[512,512]{1,0:T(8,128)(2,1)} async-done(((bf16[1024,512]{1,0:T(8,128)(2,1)}), bf16[512,512]{1,0:T(8,128)(2,1)}) %reduce-scatter.9.cloned.1.call-update) | async-done | bytes 524304 | tf_op jit(solution)/shard_map/reduce_scatter | solution.py:132
  85.2 21.2 %all-gather.11.cloned.1.call-done = bf16[1024,512]{1,0:T(8,128)(2,1)} async-done(((bf16[512,512]{1,0:T(8,128)(2,1)}), bf16[1024,512]{1,0:T(8,128)(2,1)}) %all-gather.11.cloned.1.call-update) | async-done | bytes 1048592 | tf_op jit(solution)/shard_map/all_gather | solution.py:143
  106.4 13.4 %multiply_convert_fusion.3 = (bf16[1024,1024]{1,0:T(8,128)(2,1)S(1)}, f32[1024,1024]{1,0:T(8,128)}, f32[1024,1024]{1,0:T(8,128)}) fusion(f32[1024]{0:T(1024)S(1)} %bitcast.419, bf16[1024,512]{1,0:T(8,128)(2,1)} %all-gather.11.cloned.1.call-done, bf16[2,512,1024]{2,1,0:T(8,128)(2,1)} %param.33), kind=kOutput, calls=%fused_computation.135 | convolution fusion | flops 1142947840 | bytes 12587008 | tf_op jit(solution)/shard_map/dot_general | solution.py:145
  123.6 20.4 %reduce-scatter.11.cloned.1.call-done = bf16[512,512]{1,0:T(8,128)(2,1)} async-done(((bf16[1024,512]{1,0:T(8,128)(2,1)}), bf16[512,512]{1,0:T(8,128)(2,1)}) %reduce-scatter.11.cloned.1.call-update) | async-done | bytes 524304 | tf_op jit(solution)/shard_map/reduce_scatter | solution.py:150
  147.4 21.0 %all-gather.13.cloned.1.call-done = bf16[1024,512]{1,0:T(8,128)(2,1)} async-done(((bf16[512,512]{1,0:T(8,128)(2,1)}), bf16[1024,512]{1,0:T(8,128)(2,1)}) %all-gather.13.cloned.1.call-update) | async-done | bytes 1048592 | tf_op jit(solution)/shard_map/all_gather | solution.py:121
  176.8 15.0 %while.57 = (s32[]{:T(128)}, bf16[2,512,4,64]{1,3,2,0:T(8,128)(2,1)S(1)}, f32[2,4,512]{2,1,0:T(4,128)S(1)}, s32[2,512]{1,0:T(2,128)S(1)}, bf16[2,512,4,64]{1,3,2...) while((s32[]{:T(128)}, ...), condition=%wide.region_13.14_spmd.clone, body=%wide.region_10.13_spmd.clone.sunk | while | flops 562561024 | bytes 29177976 | solution.py:48
  195.7 20.5 %reduce-scatter.13.cloned.1.call-done = bf16[512,512]{1,0:T(8,128)(2,1)} async-done(((bf16[1024,512]{1,0:T(8,128)(2,1)}), bf16[512,512]{1,0:T(8,128)(2,1)}) %reduce-scatter.13.cloned.1.call-update) | async-done | bytes 524304 | tf_op jit(solution)/shard_map/reduce_scatter | solution.py:132
  219.5 21.0 %all-gather.15.cloned.1.call-done = bf16[1024,512]{1,0:T(8,128)(2,1)} async-done(((bf16[512,512]{1,0:T(8,128)(2,1)}), bf16[1024,512]{1,0:T(8,128)(2,1)}) %all-gather.15.cloned.1.call-update) | async-done | bytes 1048592 | tf_op jit(solution)/shard_map/all_gather | solution.py:143
  240.5 13.4 %multiply_convert_fusion.2 = (bf16[1024,1024]{1,0:T(8,128)(2,1)S(1)}, f32[1024,1024]{1,0:T(8,128)}, f32[1024,1024]{1,0:T(8,128)}) fusion(f32[1024]{0:T(1024)S(1)} %bitcast.422, bf16[1024,512]{1,0:T(8,128)(2,1)} %all-gather.15.cloned.1.call-done, bf16[2,512,1024]{2,1,0:T(8,128)(2,1)} %param.33), kind=kOutput, calls=%fused_computation.122 | convolution fusion | flops 1142947840 | bytes 12587008 | tf_op jit(solution)/shard_map/dot_general | solution.py:145
  257.5 20.5 %reduce-scatter.15.cloned.1.call-done = bf16[512,512]{1,0:T(8,128)(2,1)} async-done(((bf16[1024,512]{1,0:T(8,128)(2,1)}), bf16[512,512]{1,0:T(8,128)(2,1)}) %reduce-scatter.15.cloned.1.call-update) | async-done | bytes 524304 | tf_op jit(solution)/shard_map/reduce_scatter | solution.py:150
  286.9 21.4 %all-gather.17.cloned.1.call-done = bf16[1024,512]{1,0:T(8,128)(2,1)} async-done(((bf16[512,512]{1,0:T(8,128)(2,1)}), bf16[1024,512]{1,0:T(8,128)(2,1)}) %all-gather.17.cloned.1.call-update) | async-done | bytes 1048592 | tf_op jit(solution)/shard_map/all_gather | solution.py:209
  308.3 7.3 convert_reduce_fusion
  319.4 20.3 %reduce-scatter.17.cloned.1.call-done = bf16[512,512]{1,0:T(8,128)(2,1)} async-done(((bf16[1024,512]{1,0:T(8,128)(2,1)}), bf16[512,512]{1,0:T(8,128)(2,1)}) %reduce-scatter.17.cloned.1.call-update) | async-done | bytes 524304 | tf_op jit(solution)/shard_map/reduce_scatter | solution.py:222
  345.5 21.2 %all-gather.19.cloned.1.call-done = bf16[1024,512]{1,0:T(8,128)(2,1)} async-done(((bf16[512,512]{1,0:T(8,128)(2,1)}), bf16[1024,512]{1,0:T(8,128)(2,1)}) %all-gather.19.cloned.1.call-update) | async-done | bytes 1048592 | tf_op jit(solution)/shard_map/all_gather | solution.py:233
  372.3 24.9 %while.58 = (s32[]{:T(128)}, f32[1024,4,64]{0,2,1:T(8,128)S(1)}, f32[1024,4,64]{0,2,1:T(8,128)}, bf16[2,512,4,64]{1,3,2,0:T(8,128)(2,1)}, bf16[2,512,4,64]{1,3,2...) while((s32[]{:T(128)}, f32[1024,4,64]{0,2,1:T(8,128)S(1)}, ...), condition=%wide.region_27.28_spmd.clone, body=%wide.region_25.27_spmd.clone.sunk | while | flops 1375600640 | bytes 85006632 | solution.py:92
  403.3 3.4 bitcast_convert_fusion.1
  406.8 20.5 %reduce-scatter.19.cloned.1.call-done = bf16[512,512]{1,0:T(8,128)(2,1)} async-done(((bf16[1024,512]{1,0:T(8,128)(2,1)}), bf16[512,512]{1,0:T(8,128)(2,1)}) %reduce-scatter.19.cloned.1.call-update) | async-done | bytes 524304 | tf_op jit(solution)/shard_map/reduce_scatter | solution.py:255
  432.2 21.4 %all-gather.21.cloned.1.call-done = bf16[1024,512]{1,0:T(8,128)(2,1)} async-done(((bf16[512,512]{1,0:T(8,128)(2,1)}), bf16[1024,512]{1,0:T(8,128)(2,1)}) %all-gather.21.cloned.1.call-update) | async-done | bytes 1048592 | tf_op jit(solution)/shard_map/all_gather | solution.py:209
  453.6 6.7 convert_reduce_fusion.1
  464.1 20.5 %reduce-scatter.21.cloned.1.call-done = bf16[512,512]{1,0:T(8,128)(2,1)} async-done(((bf16[1024,512]{1,0:T(8,128)(2,1)}), bf16[512,512]{1,0:T(8,128)(2,1)}) %reduce-scatter.21.cloned.1.call-update) | async-done | bytes 524304 | tf_op jit(solution)/shard_map/reduce_scatter | solution.py:222
  490.1 4.5 convolution_bitcast_fusion
  494.6 4.4 convolution_bitcast_fusion.2
  501.2 10.3 %all-gather.23.cloned.1.call-done = bf16[1024,512]{1,0:T(8,128)(2,1)} async-done(((bf16[512,512]{1,0:T(8,128)(2,1)}), bf16[1024,512]{1,0:T(8,128)(2,1)}) %all-gather.23.cloned.1.call-update) | async-done | bytes 1048592 | tf_op jit(solution)/shard_map/all_gather | solution.py:233
  519.5 26.3 %while.59 = (s32[]{:T(128)}, f32[1024,4,64]{0,2,1:T(8,128)S(1)}, f32[1024,4,64]{0,2,1:T(8,128)}, bf16[2,512,4,64]{1,3,2,0:T(8,128)(2,1)}, bf16[2,512,4,64]{1,3,2...) while((s32[]{:T(128)}, f32[1024,4,64]{0,2,1:T(8,128)S(1)}, ...), condition=%wide.region_36.37_spmd.clone, body=%wide.region_34.36_spmd.clone.sunk | while | flops 1375600640 | bytes 85006632 | solution.py:92
  551.6 3.5 bitcast_convert_fusion
  572.6 41.4 %all-reduce = (f32[2,512]{1,0:T(2,128)}, f32[2,512]{1,0:T(2,128)}, f32[2,512]{1,0:T(2,128)}, f32[2,512]{1,0:T(2,128)}, f32[2,512]{1,0:T(2,128)}, /*index=5*/f32[2,512]{1,0:T(2,128)}) all-reduce(f32[2,512]{1,0:T(2,128)S(1)} %pad_maximum_fusion.11, ...), channel_id=1, replica_groups=mesh['wide'=16,'narrow'=2] {'wide','narrow'}, use_global_device_ids=true, to_apply=%region_48.49 | all-reduce | flops 6144 | bytes 49152 | tf_op jit(solution)/shard_map/psum | solution.py:371
  614.4 63.6 %all-reduce.1 = (f32[2,256]{1,0:T(2,128)}, f32[2,256]{1,0:T(2,128)}, f32[2,1024]{1,0:T(2,128)}) all-reduce(f32[2,256]{1,0:T(2,128)S(1)} %pad_maximum_fusion.17, f32[2,256]{1,0:T(2,128)S(1)} %pad_maximum_fusion.18, f32[2,1024]{1,0:T(2,128)S(1)} %pad_maximum_fusion.10), channel_id=1, replica_groups=mesh['wide'=16,'narrow'=2] {'wide'}, use_global_device_ids=true, to_apply=%region_41.42 | all-reduce | flops 3072 | bytes 24576 | tf_op jit(solution)/shard_map/psum | solution.py:359
  680.1 135.0 %all-reduce.5.cloned.1.call-done = (f32[2,512,3,256]{1,3,2,0:T(8,128)}, f32[2,256,512]{2,1,0:T(8,128)}, f32[2,512,1024]{2,1,0:T(8,128)}, f32[2,1024,512]{2,1,0:T(8,128)}) async-done(((f32[2,512,3,256]{1,3,2,0:T(8,128)}, f32[2,256,512]{2,1,0:T(8,128)}, f32[2,512,1024]{2,1,0:T(8,128)}, f32[2,1024,512]{2,1,0:T(8,128)}), (f32[2,512,3,256]{1,3,2,0:T(8,128)}, f32[2,256,512]{2,1,0:T(8,128)}, ...) | async-done | bytes 12582928 | tf_op jit(solution)/shard_map/psum | solution.py:359
  815.1 3.6 copy.73
  819.7 4.9 copy.148
  (451 shorter events, 206.7 us)
Async XLA Ops:
  7.2 26.4 %all-gather.9.cloned.1.call-start = ((), (), s32[]{:S(2)}) async-start(), calls=%async_computation.8 | async-start | bytes 1572864 | tf_op jit(solution)/shard_map/all_gather | solution.py:121
  7.9 72.2 %reduce-scatter.9.cloned.1.call-start = ((), (), s32[]{:S(2)}) async-start(), calls=%async_computation.9 | async-start | bytes 1572864 | tf_op jit(solution)/shard_map/reduce_scatter | solution.py:132
  56.6 28.3 %copy-start = (bf16[1024,4,64]{0,2,1:T(8,128)(2,1)}, bf16[1024,4,64]{0,2,1:T(8,128)(2,1)S(1)}, u32[]{:S(2)}) copy-start(bf16[1024,4,64]{0,2,1:T(8,128)(2,1)S(1)} %get-tuple-element.1001) | copy-start | bytes 1572868
  56.6 28.3 %copy-start.2 = (bf16[2,512,4,64]{1,3,2,0:T(8,128)(2,1)}, bf16[2,512,4,64]{1,3,2,0:T(8,128)(2,1)S(1)}, u32[]{:S(2)}) copy-start(bf16[2,512,4,64]{1,3,2,0:T(8,128)(2,1)S(1)} %get-tuple-element.1003) | copy-start | bytes 1572868
  56.6 28.3 %copy-start.8 = (bf16[1024,4,64]{0,2,1:T(8,128)(2,1)}, bf16[1024,4,64]{0,2,1:T(8,128)(2,1)S(1)}, u32[]{:S(2)}) copy-start(bf16[1024,4,64]{0,2,1:T(8,128)(2,1)S(1)} %get-tuple-element.1007) | copy-start | bytes 1572868
  59.5 46.9 %all-gather.11.cloned.1.call-start = ((), (), s32[]{:S(2)}) async-start(), calls=%async_computation.10 | async-start | bytes 1572864 | tf_op jit(solution)/shard_map/all_gather | solution.py:143
  59.6 84.3 %copy-start.59 = (f32[1,512]{1,0:T(1,128)}, f32[1,512]{1,0:T(1,128)S(1)}, u32[]{:S(2)}) copy-start(f32[1,512]{1,0:T(1,128)S(1)} %get-tuple-element.570) | copy-start | bytes 6148
  59.7 84.3 %copy-start.71 = (f32[1,512]{1,0:T(1,128)}, f32[1,512]{1,0:T(1,128)S(1)}, u32[]{:S(2)}) copy-start(f32[1,512]{1,0:T(1,128)S(1)} %get-tuple-element.567) | copy-start | bytes 6148
  81.4 62.6 %copy-start.63 = (f32[512]{0:T(512)}, f32[512]{0:T(512)S(1)}, u32[]{:S(2)}) copy-start(f32[512]{0:T(512)S(1)} %broadcast_multiply_fusion.3) | copy-start | bytes 6148
  82.7 37.0 %copy-start.73 = (f32[512]{0:T(512)}, f32[512]{0:T(512)S(1)}, u32[]{:S(2)}) copy-start(f32[512]{0:T(512)S(1)} %multiply_reduce_fusion.11) | copy-start | bytes 6148
  82.8 61.2 %copy-start.69 = (f32[512]{0:T(512)}, f32[512]{0:T(512)S(1)}, u32[]{:S(2)}) copy-start(f32[512]{0:T(512)S(1)} %fusion.157) | copy-start | bytes 6148
  84.9 59.0 %reduce-scatter.11.cloned.1.call-start = ((), (), s32[]{:S(2)}) async-start(), calls=%async_computation.11 | async-start | bytes 1572864 | tf_op jit(solution)/shard_map/reduce_scatter | solution.py:150
  85.2 34.6 %copy-start.92 = (f32[1,1024]{1,0:T(1,128)}, f32[1,1024]{1,0:T(1,128)S(1)}, u32[]{:S(2)}) copy-start(f32[1,1024]{1,0:T(1,128)S(1)} %get-tuple-element.561) | copy-start | bytes 12292
  123.4 44.9 %all-gather.13.cloned.1.call-start = ((), (), s32[]{:S(2)}) async-start(), calls=%async_computation.12 | async-start | bytes 1572864 | tf_op jit(solution)/shard_map/all_gather | solution.py:121
  123.5 92.7 %copy-start.67 = (f32[1,512]{1,0:T(1,128)}, f32[1,512]{1,0:T(1,128)S(1)}, u32[]{:S(2)}) copy-start(f32[1,512]{1,0:T(1,128)S(1)} %get-tuple-element.563) | copy-start | bytes 6148
  145.6 70.6 %copy-start.4 = (f32[512,512]{1,0:T(8,128)}, f32[512,512]{1,0:T(8,128)S(1)}, u32[]{:S(2)}) copy-start(f32[512,512]{1,0:T(8,128)S(1)} %get-tuple-element.542) | copy-start | bytes 3145732
  145.6 70.6 %copy-start.61 = (f32[512]{0:T(512)}, f32[512]{0:T(512)S(1)}, u32[]{:S(2)}) copy-start(f32[512]{0:T(512)S(1)} %broadcast_multiply_fusion.2) | copy-start | bytes 6148
  145.9 70.4 %copy-start.65 = (f32[512]{0:T(512)}, f32[512]{0:T(512)S(1)}, u32[]{:S(2)}) copy-start(f32[512]{0:T(512)S(1)} %fusion.158) | copy-start | bytes 6148
  146.9 69.3 %reduce-scatter.13.cloned.1.call-start = ((), (), s32[]{:S(2)}) async-start(), calls=%async_computation.13 | async-start | bytes 1572864 | tf_op jit(solution)/shard_map/reduce_scatter | solution.py:132
  195.7 44.8 %all-gather.15.cloned.1.call-start = ((), (), s32[]{:S(2)}) async-start(), calls=%async_computation.14 | async-start | bytes 1572864 | tf_op jit(solution)/shard_map/all_gather | solution.py:143
  219.1 58.9 %reduce-scatter.15.cloned.1.call-start = ((), (), s32[]{:S(2)}) async-start(), calls=%async_computation.15 | async-start | bytes 1572864 | tf_op jit(solution)/shard_map/reduce_scatter | solution.py:150
  257.4 50.8 %all-gather.17.cloned.1.call-start = ((), (), s32[]{:S(2)}) async-start(), calls=%async_computation.16 | async-start | bytes 1572864 | tf_op jit(solution)/shard_map/all_gather | solution.py:209
  286.8 52.9 %reduce-scatter.17.cloned.1.call-start = ((), (), s32[]{:S(2)}) async-start(), calls=%async_computation.17 | async-start | bytes 1572864 | tf_op jit(solution)/shard_map/reduce_scatter | solution.py:222
  319.2 47.5 %all-gather.19.cloned.1.call-start = ((), (), s32[]{:S(2)}) async-start(), calls=%async_computation.18 | async-start | bytes 1572864 | tf_op jit(solution)/shard_map/all_gather | solution.py:233
  345.3 82.0 %reduce-scatter.19.cloned.1.call-start = ((), (), s32[]{:S(2)}) async-start(), calls=%async_computation.19 | async-start | bytes 1572864 | tf_op jit(solution)/shard_map/reduce_scatter | solution.py:255
  406.7 46.8 %copy-start.93 = (f32[1,1024]{1,0:T(1,128)S(1)}, f32[1,1024]{1,0:T(1,128)}, u32[]{:S(2)}) copy-start(f32[1,1024]{1,0:T(1,128)} %copy-done.92) | copy-start | bytes 12292
  406.8 46.8 %all-gather.21.cloned.1.call-start = ((), (), s32[]{:S(2)}) async-start(), calls=%async_computation.20 | async-start | bytes 1572864 | tf_op jit(solution)/shard_map/all_gather | solution.py:209
  432.1 52.4 %reduce-scatter.21.cloned.1.call-start = ((), (), s32[]{:S(2)}) async-start(), calls=%async_computation.21 | async-start | bytes 1572864 | tf_op jit(solution)/shard_map/reduce_scatter | solution.py:222
  464.0 47.5 %all-gather.23.cloned.1.call-start = ((), (), s32[]{:S(2)}) async-start(), calls=%async_computation.22 | async-start | bytes 1572864 | tf_op jit(solution)/shard_map/all_gather | solution.py:233
  490.0 187.9 %reduce-scatter.23.cloned.1.call-start = ((), (), s32[]{:S(2)}) async-start(), calls=%async_computation.23 | async-start | bytes 1572864 | tf_op jit(solution)/shard_map/reduce_scatter | solution.py:255
  555.2 259.9 %all-reduce.5.cloned.1.call-start = ((), (), s32[]{:S(2)}) async-start(), calls=%async_computation.24 | async-start | bytes 25165824 | tf_op jit(solution)/shard_map/psum | solution.py:359
  571.2 106.8 %copy-start.17 = (f32[512,512]{1,0:T(8,128)S(1)}, f32[512,512]{1,0:T(8,128)}, u32[]{:S(2)}) copy-start(f32[512,512]{1,0:T(8,128)} %copy-done.16) | copy-start | bytes 3145732
  (94 other events, 756.9 us)
Sparse Core Ops, SparseCore 0:
  9.5 23.9 all-gather.8
  59.7 20.3 reduce-scatter.8
  85.1 21.2 all-gather.10
  123.5 20.3 reduce-scatter.10
  147.1 21.2 all-gather.12
  195.8 20.3 reduce-scatter.12
  219.2 21.2 all-gather.14
  257.6 20.3 reduce-scatter.14
  287.0 21.2 all-gather.16
  319.3 20.3 reduce-scatter.16
  345.4 21.2 all-gather.18
  406.9 20.3 reduce-scatter.18
  432.3 21.2 all-gather.20
  464.1 20.3 reduce-scatter.20
  490.2 21.2 all-gather.22
  555.3 20.3 reduce-scatter.22
  581.2 233.8 all-reduce.4
where the time goes:
time: 841 us; the launch traced here: 833 us
  waiting for transfers between devices  440 us (52%)
  matrix products  144 us (17%)
  blocking collectives  105 us (12%)
  other arithmetic  75.3 us (9%)
  local copies, waits for them, and re-layouts  50 us (6%)
  between operations  16.7 us (2%)
    psum x1, waiting for transfers between devices, local(): lax.psum((grad_input, grad_query, grad_value, grad_output, grad_expand, g...  135 us
    psum x1, blocking collectives, local(): lax.psum((grad_input, grad_query, grad_value, grad_output, grad_expand, g...  63.6 us
    all_gather x2, waiting for transfers between devices, forward_layer(): lax.all_gather(hidden.astype(jnp.bfloat16), 'narrow', axis=0, tiled=True)  44.4 us
    all_gather x2, waiting for transfers between devices, backward_layer(): lax.all_gather(widened_grad.astype(jnp.bfloat16), 'narrow', axis=0, tiled...  42.8 us
    all_gather x2, waiting for transfers between devices, forward_layer(): lax.all_gather(normed.astype(jnp.bfloat16), 'narrow', axis=0, tiled=True)  42.2 us
    psum x1, blocking collectives, local(): lax.psum((grad_output_bias, grad_first_gain, grad_first_shift, grad_shrin...  41.4 us
    reduce_scatter x2, waiting for transfers between devices, forward_layer(): lax.psum_scatter(jnp.dot(activated, shrink_weight, preferred_element_type...  40.9 us
    reduce_scatter x2, waiting for transfers between devices, forward_layer(): lax.psum_scatter(jnp.dot(mixed_low, output_weight, preferred_element_type...  40.9 us
  transfers between devices with their start and end apart: 17, of which 16 were waited for; matrix products, arithmetic and copies ran while one was open for 4% of the time, Pallas kernels for 0%

commit v1 on v0

v1 whole, which is shorter than its diff:
```python
import functools

import jax
import jax.numpy as jnp
from jax import lax
from jax.experimental import pallas as pl
from jax.experimental.pallas import tpu as pltpu
from jax.sharding import PartitionSpec as P

DH = 64
EPSILON = 1e-12
MASKED = -1e9
AXES = ("wide", "narrow")
F32 = jnp.float32
BF16 = jnp.bfloat16
LAYER_VECTORS = 6


def dot(a, b):
    return lax.dot_general(a, b, (((1,), (0,)), ((), ())), preferred_element_type=F32)


def dot_rt(a, b):
    return lax.dot_general(a, b, (((1,), (1,)), ((), ())), preferred_element_type=F32)


def dot_lt(a, b):
    return lax.dot_general(a, b, (((0,), (0,)), ((), ())), preferred_element_type=F32)


def start_quarters(own, mine, theirs, buffer, sem, core):
    own_one, own_two = own
    copies = (
        pltpu.make_async_copy(own_one, buffer.at[0], sem.at[0]),
        pltpu.make_async_copy(mine, buffer.at[1], sem.at[1]),
        pltpu.make_async_copy(own_two, buffer.at[2], sem.at[2]),
        pltpu.make_async_copy(theirs, buffer.at[3], sem.at[3]),
    )
    for copy in copies:
        copy.start()
    return copies


def finish(copies):
    for copy in copies:
        copy.wait()


def lane_halves(shape):
    lane = lax.broadcasted_iota(jnp.int32, shape, len(shape) - 1)
    return lane < DH


def normalise(x):
    centre = x - jnp.mean(x, -1, keepdims=True)
    scale = lax.rsqrt(jnp.mean(centre * centre, -1, keepdims=True) + EPSILON)
    return centre * scale, scale


def gelu_parts(a):
    square = jnp.exp(-0.5 * a * a)
    size = jnp.abs(a)
    t = 1.0 / (1.0 + (0.3275911 * 0.7071067811865476) * size)
    poly = t * (
        0.127414796
        + t * (-0.142248368 + t * (0.7107068705 + t * (-0.7265760135 + t * 0.5307027145)))
    )
    tail = poly * square
    phi = jnp.where(a >= 0, 1.0 - tail, tail)
    return a * phi, phi + a * square * 0.3989422804014327


def project(hidden_low, weight, query_bias, value_bias, query_ref, pair_ref):
    def one(index, carry):
        triple = dot(hidden_low, weight[index])
        width = triple.shape[1] // 3
        query = (triple[:, :width] + query_bias[index]).astype(BF16)
        query_ref[index] = query * BF16(DH ** (-0.5))
        pair_ref[index, :, :width] = triple[:, width : 2 * width].astype(BF16)
        pair_ref[index, :, width:] = (triple[:, 2 * width :] + value_bias[index]).astype(BF16)
        return carry

    lax.fori_loop(0, 4, one, 0)


def first_kernel(tokens, weight_own, weight_mine, weight_theirs, query_bias, value_bias, query_ref, pair_ref, buffer, sem):
    core = lax.rem(lax.axis_index("wide"), 2)
    copies = start_quarters(
        (weight_own.at[core], weight_own.at[1 - core]), weight_mine, weight_theirs, buffer, sem, core
    )
    finish(copies)
    project(tokens[...], buffer, query_bias, value_bias, query_ref, pair_ref)


def forward_kernel(layer, last, *refs):
    (bias, query, pair, remote, hidden, wo_own, wo_mine, wo_theirs, we_own, we_mine, we_theirs, ws_own, ws_mine, ws_theirs, vectors, expand_bias), refs = refs[:16], refs[16:]
    if not last:
        (wi_own, wi_mine, wi_theirs, query_bias, value_bias), refs = refs[:5], refs[5:]
    (mixed_ref, total_ref, normed_ref, first_ref, first_scale, active_ref, slope_ref, second_ref, second_scale, hidden_ref), refs = refs[:10], refs[10:]
    if not last:
        (low_ref, query_ref, pair_ref), refs = refs[:3], refs[3:]
    (wo, we, ws, acc, sem), refs = refs[:5], refs[5:]
    core = lax.rem(lax.axis_index("wide"), 2)
    units = we.shape[2]
    wo_copies = start_quarters((wo_own.at[layer, core], wo_own.at[layer, 1 - core]), wo_mine, wo_theirs, wo, sem.at[0], core)

    def columns(index):
        return we_own.at[layer, :, pl.ds(pl.multiple_of(index * units, 128), units)]

    we_copies = start_quarters((columns(core), columns(1 - core)), we_mine, we_theirs, we, sem.at[1], core)
    ws_copies = start_quarters((ws_own.at[layer, core], ws_own.at[layer, 1 - core]), ws_mine, ws_theirs, ws, sem.at[2], core)
    if not last:
        wi = refs[0]
        wi_copies = start_quarters((wi_own.at[core], wi_own.at[1 - core]), wi_mine, wi_theirs, wi, sem.at[3], core)
    shift = bias[0]
    rows, width = query.shape[1], query.shape[2]
    acc[...] = hidden[...] + vectors[0:1]
    finish(wo_copies)
    halves = lane_halves((rows, width))

    def one_pair(index, carry):
        there = lax.rem(index + 2, 4)
        queries = query[index]
        key_here, value_here = pair[index, :, :width], pair[index, :, width:]
        key_there, value_there = remote[there, :, :width], remote[there, :, width:]
        mixed, total = [], []
        for part in range(2):
            mask = halves if part == 0 else jnp.logical_not(halves)
            masked = jnp.where(mask, queries, BF16(0))
            here = dot_rt(masked, key_here)
            away = dot_rt(masked, key_there)
            peak = jnp.maximum(jnp.max(here, -1, keepdims=True), jnp.max(away, -1, keepdims=True) + shift)
            here = jnp.exp(here - peak)
            away = jnp.exp(away - (peak - shift))
            weight = jnp.sum(here, -1, keepdims=True) + jnp.sum(away, -1, keepdims=True)
            both = dot(here.astype(BF16), value_here) + dot(away.astype(BF16), value_there)
            mixed.append(both * (1.0 / weight))
            total.append(jnp.broadcast_to(peak + jnp.log(weight), (rows, width)))
        low = jnp.where(halves, mixed[0], mixed[1]).astype(BF16)
        mixed_ref[index] = low
        totals = jnp.where(halves, total[0], total[1]).T
        total_ref[index] = jnp.concatenate([totals[0:8], totals[DH : DH + 8]], 0)
        acc[...] += dot(low, wo[index])
        return carry

    lax.fori_loop(0, 4, one_pair, 0)
    first, scale = normalise(acc[...])
    first_ref[...] = first
    first_scale[...] = scale
    normed = first * vectors[1:2] + vectors[2:3]
    normed_low = normed.astype(BF16)
    normed_ref[...] = normed_low
    acc[...] = normed + vectors[3:4]
    finish(we_copies)
    finish(ws_copies)

    def one_quarter(index, carry):
        active, slope = gelu_parts(dot(normed_low, we[index]) + expand_bias[index])
        low = active.astype(BF16)
        active_ref[index] = low
        slope_ref[index] = slope.astype(BF16)
        acc[...] += dot(low, ws[index])
        return carry

    lax.fori_loop(0, 4, one_quarter, 0)
    second, scale = normalise(acc[...])
    second_ref[...] = second
    second_scale[...] = scale
    result = second * vectors[4:5] + vectors[5:6]
    hidden_ref[...] = result
    if not last:
        low_ref[...] = result.astype(BF16)
        finish(wi_copies)
        project(low_ref[...], wi, query_bias, value_bias, query_ref, pair_ref)


def column_sum(x):
    return jnp.sum(x, 0, keepdims=True)


def norm_backward(grad, normed, scale, gain):
    scaled = grad * gain
    return (
        scaled - jnp.mean(scaled, -1, keepdims=True) - normed * jnp.mean(scaled * normed, -1, keepdims=True)
    ) * scale


def block_kernel(layer, *refs):
    (grad, second, second_scale, active, slope, normed, first, first_scale, mixed, vectors, wo_own, wo_mine, wo_theirs, we_own, we_mine, we_theirs, ws_own, ws_mine, ws_theirs), refs = refs[:19], refs[19:]
    (shrink_ref, expand_ref, output_ref, summed_ref, mixed_grad_ref, inner_ref, vector_ref, expand_bias_ref), refs = refs[:8], refs[8:]
    wo, we, ws, acc, turned, sem = refs
    core = lax.rem(lax.axis_index("wide"), 2)
    units = we.shape[2]
    ws_copies = start_quarters((ws_own.at[layer, core], ws_own.at[layer, 1 - core]), ws_mine, ws_theirs, ws, sem.at[2], core)

    def columns(index):
        return we_own.at[layer, :, pl.ds(pl.multiple_of(index * units, 128), units)]

    we_copies = start_quarters((columns(core), columns(1 - core)), we_mine, we_theirs, we, sem.at[1], core)
    wo_copies = start_quarters((wo_own.at[layer, core], wo_own.at[layer, 1 - core]), wo_mine, wo_theirs, wo, sem.at[0], core)
    rows, width = mixed.shape[1], mixed.shape[2]
    incoming = grad[...].astype(F32)
    widened = norm_backward(incoming, second[...], second_scale[...], vectors[4:5])
    vector_ref[0:1] = column_sum(incoming)
    vector_ref[1:2] = column_sum(incoming * second[...])
    vector_ref[2:3] = column_sum(widened)
    acc[...] = widened
    branch = widened.astype(BF16)
    turned[...] = normed[...].T
    finish(ws_copies)
    finish(we_copies)

    def one_quarter(index, carry):
        active_grad = dot_rt(branch, ws[index])
        inner = (active_grad * slope[index].astype(F32)).astype(BF16)
        shrink_ref[index] = dot_lt(active[index], branch).astype(BF16)
        expand_ref[index] = dot(turned[...], inner).astype(BF16)
        expand_bias_ref[index] = jnp.broadcast_to(column_sum(inner.astype(F32)), expand_bias_ref.shape[1:])
        acc[...] += dot_rt(inner, we[index])
        return carry

    lax.fori_loop(0, 4, one_quarter, 0)
    outgoing = acc[...]
    summed = norm_backward(outgoing, first[...], first_scale[...], vectors[1:2])
    vector_ref[3:4] = column_sum(outgoing)
    vector_ref[4:5] = column_sum(outgoing * first[...])
    vector_ref[5:6] = column_sum(summed)
    vector_ref[6:8] = jnp.zeros((2, summed.shape[1]), F32)
    summed_ref[...] = summed
    low = summed.astype(BF16)
    finish(wo_copies)
    half = lax.broadcasted_iota(jnp.int32, (16, width), 1) // DH
    which = lax.broadcasted_iota(jnp.int32, (16, width), 0) // 8
    selector = (half == which).astype(F32)

    def one_pair(index, carry):
        mixed_grad = dot_rt(low, wo[index]).astype(BF16)
        mixed_grad_ref[index] = mixed_grad
        output_ref[index] = dot_lt(mixed[index], low).astype(BF16)
        product = mixed_grad.astype(F32) * mixed[index].astype(F32)
        inner_ref[index] = lax.dot_general(
            selector, product, (((1,), (1,)), ((), ())), precision=lax.Precision.HIGHEST, preferred_element_type=F32
        )
        return carry

    lax.fori_loop(0, 4, one_pair, 0)


def attention_kernel(bias, query, pair, remote, mixed_grad, total, inner, query_grad_ref, here_ref, away_ref):
    rows, width = query.shape[1], query.shape[2]
    halves = lane_halves((rows, width))
    shift = bias[0]

    def one_pair(index, carry):
        there = lax.rem(index + 2, 4)
        queries, grads = query[index], mixed_grad[index]
        turned = None
        for side in range(2):
            source, place = (pair, index) if side == 0 else (remote, there)
            keys, values = source[place, :, :width], source[place, :, width:]
            key_grad = value_grad = None
            for part in range(2):
                mask = halves if part == 0 else jnp.logical_not(halves)
                masked_query = jnp.where(mask, queries, BF16(0))
                masked_grad = jnp.where(mask, grads, BF16(0))
                masked_key = jnp.where(mask, keys, BF16(0))
                level = total[index, 8 * part : 8 * part + 1]
                if side == 1:
                    level = level - shift
                weights = jnp.exp(dot_rt(keys, masked_query) - level)
                update = dot(weights.astype(BF16), masked_grad)
                value_grad = update if value_grad is None else value_grad + update
                slopes = dot_rt(values, masked_grad) - inner[index, 8 * part : 8 * part + 1]
                slopes = (weights * slopes).astype(BF16)
                update = dot(slopes, masked_query)
                key_grad = update if key_grad is None else key_grad + update
                update = dot_lt(masked_key, slopes)
                turned = update if turned is None else turned + update
            if side == 0:
                here_ref[index, :, :width] = key_grad
                here_ref[index, :, width:] = value_grad
            else:
                away_ref[there, :, :width] = key_grad.astype(BF16)
                away_ref[there, :, width:] = value_grad.astype(BF16)
        query_grad_ref[index] = (turned * DH ** (-0.5)).T.astype(BF16)
        return carry

    lax.fori_loop(0, 4, one_pair, 0)


def input_kernel(query_grad, here, away, hidden_low, summed, wi_own, wi_mine, wi_theirs, weight_ref, grad_ref, query_bias_ref, value_bias_ref, wi, turned, acc, sem):
    core = lax.rem(lax.axis_index("wide"), 2)
    copies = start_quarters((wi_own.at[core], wi_own.at[1 - core]), wi_mine, wi_theirs, wi, sem, core)
    width = query_grad.shape[2]
    turned[...] = hidden_low[...].T
    acc[...] = summed[...]
    finish(copies)

    def one(index, carry):
        pair_grad = (here[index] + away[index].astype(F32)).astype(BF16)
        triple = jnp.concatenate([query_grad[index], pair_grad], 1)
        weight_ref[index] = dot(turned[...], triple).astype(BF16)
        acc[...] += dot_rt(triple, wi[index])
        sums = column_sum(triple.astype(F32))
        query_bias_ref[index] = jnp.broadcast_to(sums[:, :width], query_bias_ref.shape[1:])
        value_bias_ref[index] = jnp.broadcast_to(sums[:, 2 * width :], value_bias_ref.shape[1:])
        return carry

    lax.fori_loop(0, 4, one, 0)
    grad_ref[...] = acc[...]


VM = pl.BlockSpec(memory_space=pltpu.VMEM)
AN = pl.BlockSpec(memory_space=pl.ANY)
SM = pl.BlockSpec(memory_space=pltpu.SMEM)


def shaped(dtype, *dims):
    return jax.ShapeDtypeStruct(dims, dtype)


def cost(flops, size):
    return pl.CostEstimate(flops=flops, bytes_accessed=size, transcendentals=0)


def call(body, name, ins, outs, scratch, args, flops=10**9):
    return pl.pallas_call(
        body,
        out_shape=outs,
        in_specs=ins,
        out_specs=[VM] * len(outs),
        scratch_shapes=scratch,
        compiler_params=pltpu.CompilerParams(vmem_limit_bytes=60 * 2**20),
        cost_estimate=cost(flops, 10**7),
        name=name,
    )(*args)


def permutations(mesh_shape):
    wide, narrow = mesh_shape
    line = lambda w, y: w * narrow + y
    every = [(w, y) for w in range(wide) for y in range(narrow)]
    swap = [(line(w, y), line((w & ~1) | y, w & 1)) for w, y in every]
    across = [(line(w, y), line(w, 1 - y)) for w, y in every]
    partner = [(line(w, y), line(w ^ 1, y)) for w, y in every]
    return swap, across, partner


def local(
    tokens, input_weight, query_bias, value_bias, output_weight, output_bias, first_gain, first_shift,
    expand_weight, expand_bias, shrink_weight, shrink_bias, second_gain, second_shift, lengths, bucket, cotangent,
):
    wide, narrow = lax.axis_size("wide"), lax.axis_size("narrow")
    assert narrow == 2 and wide % 2 == 0
    swap, across, partner = permutations((wide, narrow))
    core = lax.axis_index("wide") % 2
    send = lambda x, pairs: lax.ppermute(x, AXES, pairs)
    layers, depth = input_weight.shape[0], input_weight.shape[1]
    rows = tokens.shape[0]
    width = input_weight.shape[3] // 2
    units = expand_weight.shape[2] // 2

    tokens = send(tokens, swap)
    single = send(jnp.broadcast_to(bucket, (8, 128)).astype(F32), swap)[0, 0] < 0.5
    shift = jnp.where(single, 0.0, MASKED).astype(F32).reshape(1)

    input_own = (
        input_weight.reshape(layers, depth, 3, 2, width).transpose(0, 3, 1, 2, 4).reshape(layers, 2, depth, 3 * width)
    )
    output_own = output_weight.reshape(layers, 2, width, depth)
    shrink_own = shrink_weight.reshape(layers, 2, units, depth)
    pick = lambda x: lax.dynamic_index_in_dim(x, core, 0, keepdims=False)

    small = jnp.concatenate([query_bias, value_bias, expand_bias], 1)
    small_away = send(small, across)

    def fetch(piece):
        mine = send(piece, across)
        return mine, send(mine, partner)

    fetched = []
    for layer in range(layers):
        fetched.append((
            fetch(pick(input_own[layer])),
            fetch(pick(output_own[layer])),
            fetch(lax.dynamic_slice_in_dim(expand_weight[layer], core * units, units, 1)),
            fetch(pick(shrink_own[layer])),
        ))

    def quarters(own, away, at, size):
        own = own[:, at : at + 2 * size].reshape(layers, 2, 1, size)
        away = away[:, at : at + 2 * size].reshape(layers, 2, 1, size)
        both = jnp.stack([own, away], 2)
        both = jnp.where(core == 0, both, both[:, ::-1])
        return both.reshape(layers, 4, 1, size)

    query_biases = quarters(small, small_away, 0, width)
    value_biases = quarters(small, small_away, 2 * width, width)
    expand_biases = quarters(small, small_away, 4 * width, units)
    vectors = jnp.stack(
        [output_bias, first_gain, first_shift, shrink_bias, second_gain, second_shift, output_bias, output_bias], 1
    )

    wi_scratch = pltpu.VMEM((4, depth, 3 * width), BF16)
    wo_scratch = pltpu.VMEM((4, width, depth), BF16)
    we_scratch = pltpu.VMEM((4, depth, units), BF16)
    ws_scratch = pltpu.VMEM((4, units, depth), BF16)
    acc_scratch = pltpu.VMEM((rows, depth), F32)
    turn_scratch = pltpu.VMEM((depth, rows), BF16)
    query_shape = shaped(BF16, 4, rows, width)
    pair_shape = shaped(BF16, 4, rows, 2 * width)
    row_shape = shaped(F32, rows, depth)
    low_shape = shaped(BF16, rows, depth)
    scale_shape = shaped(F32, rows, 1)
    stat_shape = shaped(F32, 4, 16, rows)
    wide_shape = shaped(BF16, 4, rows, units)

    query, pair = call(
        first_kernel, "first",
        [VM, AN, AN, AN, VM, VM], [query_shape, pair_shape],
        [wi_scratch, pltpu.SemaphoreType.DMA((4,))],
        (tokens, input_own[0], *fetched[0][0], query_biases[0], value_biases[0]),
    )
    hidden, low = tokens.astype(F32), tokens
    saved = []
    for layer in range(layers):
        last = layer == layers - 1
        remote = send(pair, partner)
        ins = [SM, VM, VM, VM, VM] + [AN] * 9 + [VM, VM]
        args = [shift, query, pair, remote, hidden, output_own, *fetched[layer][1], expand_weight, *fetched[layer][2], shrink_own, *fetched[layer][3], vectors[layer], expand_biases[layer]]
        outs = [query_shape, stat_shape, low_shape, row_shape, scale_shape, wide_shape, wide_shape, row_shape, scale_shape, row_shape]
        scratch = [wo_scratch, we_scratch, ws_scratch, acc_scratch, pltpu.SemaphoreType.DMA((4, 4))]
        if not last:
            ins += [AN] * 3 + [VM, VM]
            args += [input_own[layer + 1], *fetched[layer + 1][0], query_biases[layer + 1], value_biases[layer + 1]]
            outs += [low_shape, query_shape, pair_shape]
            scratch += [wi_scratch]
        results = call(functools.partial(forward_kernel, layer, last), f"forward_{layer}", ins, outs, scratch, args, 5 * 10**9)
        saved.append((low, query, pair, remote) + tuple(results[:9]))
        hidden = results[9]
        if not last:
            low, query, pair = results[10:]
    layer_output = send(hidden.astype(BF16), swap).astype(F32)

    grad = send(cotangent, swap)
    collected = [None] * layers
    for layer in reversed(range(layers)):
        low, query, pair, remote, mixed, total, normed, first, first_scale, active, slope, second, second_scale = saved[layer]
        shrink_grad, expand_grad, output_grad, summed, mixed_grad, inner, vector_grad, expand_bias_grad = call(
            functools.partial(block_kernel, layer), f"block_{layer}",
            [VM] * 10 + [AN] * 9,
            [shaped(BF16, 4, units, depth), shaped(BF16, 4, depth, units), shaped(BF16, 4, width, depth), row_shape, query_shape, stat_shape, shaped(F32, 8, depth), shaped(F32, 4, 8, units)],
            [wo_scratch, we_scratch, ws_scratch, acc_scratch, turn_scratch, pltpu.SemaphoreType.DMA((3, 4))],
            (grad, second, second_scale, active, slope, normed, first, first_scale, mixed, vectors[layer], output_own, *fetched[layer][1], expand_weight, *fetched[layer][2], shrink_own, *fetched[layer][3]),
            5 * 10**9,
        )
        query_grad, here, away = call(
            attention_kernel, f"attention_{layer}",
            [SM] + [VM] * 6, [query_shape, shaped(F32, 4, rows, 2 * width), pair_shape], [],
            (shift, query, pair, remote, mixed_grad, total, inner), 5 * 10**9,
        )
        back = send(away, partner)
        input_grad, grad, query_bias_grad, value_bias_grad = call(
            input_kernel, f"input_{layer}",
            [VM] * 5 + [AN] * 3,
            [shaped(BF16, 4, depth, 3 * width), row_shape, shaped(F32, 4, 8, width), shaped(F32, 4, 8, width)],
            [wi_scratch, turn_scratch, acc_scratch, pltpu.SemaphoreType.DMA((4,))],
            (query_grad, here, back, low, summed, input_own[layer], *fetched[layer][0]), 2 * 10**9,
        )
        collected[layer] = (shrink_grad, expand_grad, output_grad, input_grad, vector_grad, expand_bias_grad, query_bias_grad, value_bias_grad)
    input_rows = send(grad.astype(BF16), swap).astype(F32)
    return reduce_all(collected, layer_output, input_rows, send, core, across, partner, wide, layers, depth, width, units)


def reduce_all(collected, layer_output, input_rows, send, core, across, partner, wide, layers, depth, width, units):
    names = list(zip(*collected))
    shrink_grad, expand_grad, output_grad, input_grad = (jnp.stack(item, 1) for item in names[:4])
    vector_grad = jnp.stack(names[4], 0)
    narrow_rows = jnp.stack(
        [jnp.concatenate([q[:, 0], v[:, 0], e[:, 0]], 1) for e, q, v in zip(names[5], names[6], names[7])], 1
    )
    same = [[w for w in range(wide) if w % 2 == c] for c in range(2)]

    def reduce_quarters(x):
        mine = (x[:2].astype(F32) + send(x[2:], partner).astype(F32)).astype(BF16)
        mine = (mine[0].astype(F32) + send(mine[1], across).astype(F32)).astype(BF16)
        return mine

    parts = [reduce_quarters(x) for x in (shrink_grad, expand_grad, output_grad, input_grad, narrow_rows.astype(BF16))]
    flat = jnp.concatenate([p.reshape(-1, 512) for p in parts], 0)
    flat = lax.psum(flat, "wide", axis_index_groups=same)
    done, at = [], 0
    for p in parts:
        size = p.size // 512
        done.append(flat[at : at + size].reshape(p.shape))
        at += size
    vector_grad = lax.psum(vector_grad, AXES)

    def spread(x):
        there = send(x, partner)
        x, there = x.astype(F32), there.astype(F32)
        return jnp.where(core == 0, x, there), jnp.where(core == 0, there, x)

    shrink_one, shrink_two = spread(done[0])
    expand_one, expand_two = spread(done[1])
    output_one, output_two = spread(done[2])
    input_one, input_two = spread(done[3])
    rows_one, rows_two = spread(done[4])
    triple = lambda x: x.reshape(layers, depth, 3, width)
    columns = lambda a, b: jnp.concatenate([rows_one[:, a:b], rows_two[:, a:b]], 1)
    return (
        layer_output,
        input_rows,
        jnp.concatenate([triple(input_one), triple(input_two)], 3),
        columns(0, width),
        columns(width, 2 * width),
        jnp.concatenate([output_one, output_two], 1),
        vector_grad[:, 5],
        vector_grad[:, 4],
        vector_grad[:, 3],
        jnp.concatenate([expand_one, expand_two], 2),
        columns(2 * width, 2 * width + units),
        jnp.concatenate([shrink_one, shrink_two], 1),
        vector_grad[:, 2],
        vector_grad[:, 1],
        vector_grad[:, 0],
    )


def solution(mesh):
    split = P(AXES, None)
    in_specs = (
        split, P(None, None, None, "narrow"), P(None, "narrow"), P(None, "narrow"), P(None, "narrow", None), P(), P(), P(),
        P(None, None, "narrow"), P(None, "narrow"), P(None, "narrow", None), P(), P(), P(), P("wide"), P("wide"), split,
    )
    out_specs = (
        split, split, P(None, None, None, "narrow"), P(None, "narrow"), P(None, "narrow"), P(None, "narrow", None), P(), P(), P(),
        P(None, None, "narrow"), P(None, "narrow"), P(None, "narrow", None), P(), P(), P(),
    )
    return jax.shard_map(local, mesh=mesh, in_specs=in_specs, out_specs=out_specs, check_vma=False)
```

time: 841 us -> 483 us (0.57)
  waiting for transfers between devices: 440 us -> 142 us
  matrix products: 144 us -> 0 us
  Pallas kernels: 0 us -> 130 us
  blocking collectives: 105 us -> 50.4 us
  other arithmetic: 75.3 us -> 40.6 us
  starting transfers between devices: 1.67 us -> 32.6 us
  local copies, waits for them, and re-layouts: 50 us -> 60.9 us
    all_gather x8 -> x0, waiting for transfers between devices: 161 us -> none  [the longest x2 44.4 us: forward_layer(): lax.all_gather(hidden.astype(jnp.bfloat16), 'narrow', axis=0, tiled=True)]
    dot_general x52 -> x0, matrix products: 144 us -> none  [the longest x2 26.7 us: forward_layer(): jnp.dot(normed_low, expand_weight, preferred_element_type=jnp.float32)]
    reduce_scatter x8 -> x0, waiting for transfers between devices: 143 us -> none  [the longest x2 40.9 us: forward_layer(): lax.psum_scatter(jnp.dot(activated, shrink_weight, preferred_element_type...]
    pallas_call x0 -> x9, Pallas kernels: none -> 130 us  [call(): pl.pallas_call(body, out_shape=outs, in_specs=ins, out_specs=[VM] * len(o...]
    ppermute x0 -> x41, waiting for transfers between devices: none -> 70.4 us  [local(): send = lambda x, pairs: lax.ppermute(x, AXES, pairs)]
    psum x1, waiting for transfers between devices: 135 us -> 72.1 us  [reduce_all(): flat = lax.psum(flat, 'wide', axis_index_groups=same)]
    psum x2 -> x1, blocking collectives: 105 us -> 50.4 us  [reduce_all(): vector_grad = lax.psum(vector_grad, AXES)]
    reduce_sum x25 -> x0, other arithmetic: 35.6 us -> none  [the longest x8 14 us: layer_norm(): centre = values - jnp.mean(values, -1, keepdims=True)]
  transfers between devices with their start and end apart: 17 -> 42, of which waited for: 16 -> 10; matrix products, arithmetic and copies ran while one was open for 4% -> 17% of each run, Pallas kernels for 0% -> 16%
where the time goes in v1:
time: 483 us; the launch traced here: 474 us
  waiting for transfers between devices  142 us (29%)
  Pallas kernels  130 us (27%)
  local copies, waits for them, and re-layouts  60.9 us (13%)
  blocking collectives  50.4 us (10%)
  other arithmetic  40.6 us (8%)
  starting transfers between devices  32.6 us (7%)
  between operations  16.6 us (3%)
    pallas_call x9, Pallas kernels, call(): pl.pallas_call(body, out_shape=outs, in_specs=ins, out_specs=[VM] * len(o...  130 us
    psum x1, waiting for transfers between devices, reduce_all(): flat = lax.psum(flat, 'wide', axis_index_groups=same)  72.1 us
    ppermute x41, waiting for transfers between devices, local(): send = lambda x, pairs: lax.ppermute(x, AXES, pairs)  70.4 us
    psum x1, blocking collectives, reduce_all(): vector_grad = lax.psum(vector_grad, AXES)  50.4 us
    ppermute x41, starting transfers between devices, local(): send = lambda x, pairs: lax.ppermute(x, AXES, pairs)  32.6 us
    unnamed x96, local copies, waits for them, and re-layouts  18.3 us
  transfers between devices with their start and end apart: 42, of which 10 were waited for; matrix products, arithmetic and copies ran while one was open for 17% of the time, Pallas kernels for 16%

profile of v1, /device:TPU:0, one launch (start us, length us, event | category | flops | bytes accessed | tf_op | source)
XLA Modules:
  0.0 474.1 jit_solution(4208239474369161542)
XLA Ops:
  11.1 3.0 collective-permute-start.4
  14.1 5.4 %collective-permute-start.1 = (bf16[512,512]{1,0:T(8,128)(2,1)}, bf16[512,512]{1,0:T(8,128)(2,1)}, u32[]{:S(2)}, u32[]{:S(2)}) collective-permute-start(bf16[512,512]{1,0:T(8,128)(2,1)} %param.17), channel_id=1, source_target_pairs={{0,0},{1,2},{2,1},{3,3},{4,4},{5,6},{6,5},{7,7},{8,8},{9,10},{10,9... | collective-permute-start | bytes 1572872 | tf_op jit(solution)/shard_map/ppermute | solution.py:357
  25.8 2.8 fusion.11
  44.7 5.5 %first.1 = (bf16[4,512,128]{2,1,0:T(8,128)(2,1)}, bf16[4,512,256]{2,1,0:T(8,128)(2,1)}) custom-call(bf16[512,512]{1,0:T(8,128)(2,1)} %collective-permute-done.1.tokens.hidden_low, bf16[2,512,384]{2,1,0:T(8,128)(2,1)} %copy.70.weight_own.wi_own, bf16[512,384]{1,0:T(8,128)(2,1)} %collective-permute-done.2.weight_mine.wi_mine, bf16[512,384]{1,0:T(8,128)(2,1)} %copy-done.32, ...), custom_call_target="tpu_custom_call" | custom-call | flops 1000000000 | bytes 10000000 | tf_op jit(solution)/shard_map/first/pallas_call | solution.py:327
  57.8 7.7 %collective-permute-done.8.refs_9_.refs_14_ = bf16[512,512]{1,0:T(8,128)(2,1)} collective-permute-done((bf16[512,512]{1,0:T(8,128)(2,1)}, bf16[512,512]{1,0:T(8,128)(2,1)}, u32[]{:S(2)}, u32[]{:S(2)}) %collective-permute-start.8) | collective-permute-done | bytes 524320 | tf_op jit(solution)/shard_map/ppermute | solution.py:357
  67.9 2.1 convert_element_type.160.refs_4_
  73.1 23.6 %forward_0.1 = (bf16[4,512,128]{2,1,0:T(8,128)(2,1)}, f32[4,16,512]{2,1,0:T(8,128)}, bf16[512,512]{1,0:T(8,128)(2,1)}, f32[512,512]{1,0:T(8,128)}, f32[512,1]{1,...) custom-call(f32[1]{0:T(128)} %bitcast.1.refs_0_.bias, ...), custom_call_target="tpu_custom_call" | custom-call | flops 5000000000 | bytes 10000000 | tf_op jit(solution)/shard_map/forward_0/pallas_call | solution.py:327
  98.3 5.0 %collective-permute-done.15.refs_6_.refs_11_ = bf16[128,512]{1,0:T(8,128)(2,1)S(1)} collective-permute-done((bf16[128,512]{1,0:T(8,128)(2,1)S(1)}, bf16[128,512]{1,0:T(8,128)(2,1)S(1)}, u32[]{:S(2)}, u32[]{:S(2)}) %collective-permute-start.15) | collective-permute-done | bytes 131104 | tf_op jit(solution)/shard_map/ppermute | solution.py:357
  106.1 20.6 %forward_1.1 = (bf16[4,512,128]{2,1,0:T(8,128)(2,1)}, f32[4,16,512]{2,1,0:T(8,128)}, bf16[512,512]{1,0:T(8,128)(2,1)}, f32[512,512]{1,0:T(8,128)}, f32[512,1]{1,...) custom-call(f32[1]{0:T(128)} %bitcast.1.refs_0_.bias, ...), custom_call_target="tpu_custom_call" | custom-call | flops 5000000000 | bytes 10000000 | tf_op jit(solution)/shard_map/forward_1/pallas_call | solution.py:327
  127.5 16.1 %block_1.1 = (bf16[4,512,512]{2,1,0:T(8,128)(2,1)}, bf16[4,512,512]{2,1,0:T(8,128)(2,1)}, bf16[4,128,512]{2,1,0:T(8,128)(2,1)}, f32[512,512]{1,0:T(8,128)}, bf16...) custom-call(bf16[512,512]{1,0:T(8,128)(2,1)} %copy-done.31, ...), custom_call_target="tpu_custom_call" | custom-call | flops 5000000000 | bytes 10000000 | tf_op jit(solution)/shard_map/block_1/pallas_call | solution.py:327
  143.6 15.8 %attention_1.1 = (bf16[4,512,128]{2,1,0:T(8,128)(2,1)}, f32[4,512,256]{2,1,0:T(8,128)}, bf16[4,512,256]{2,1,0:T(8,128)(2,1)}) custom-call(f32[1]{0:T(128)} %bitcast.1.refs_0_.bias, bf16[4,512,128]{2,1,0:T(8,128)(2,1)} %get-tuple-element.72.refs_1_.query, bf16[4,512,256]{2,1,0:T(8,128)(2,1)} %get-tuple-element.73.refs_2_.pair, ...), custom_call_target="tpu_custom_call" | custom-call | flops 5000000000 | bytes 10000000 | tf_op jit(solution)/shard_map/attention_1/pallas_call | solution.py:327
  161.1 2.5 collective-permute-done.23.away
  164.6 8.0 %input_1.1 = (bf16[4,512,384]{2,1,0:T(8,128)(2,1)}, f32[512,512]{1,0:T(8,128)}, f32[4,8,128]{2,1,0:T(8,128)}, f32[4,8,128]{2,1,0:T(8,128)}) custom-call(bf16[4,512,128]{2,1,0:T(8,128)(2,1)} %get-tuple-element.87.query_grad, f32[4,512,256]{2,1,0:T(8,128)} %get-tuple-element.88.here, bf16[4,512,256]{2,1,0:T(8,128)(2,1)} %copy-done.25, ...), custom_call_target="tpu_custom_call" | custom-call | flops 2000000000 | bytes 10000000 | tf_op jit(solution)/shard_map/input_1/pallas_call | solution.py:327
  172.6 16.6 %block_0.1 = (bf16[4,512,512]{2,1,0:T(8,128)(2,1)}, bf16[4,512,512]{2,1,0:T(8,128)(2,1)}, bf16[4,128,512]{2,1,0:T(8,128)(2,1)}, f32[512,512]{1,0:T(8,128)}, bf16...) custom-call(f32[512,512]{1,0:T(8,128)} %get-tuple-element.92.refs_0_, ...), custom_call_target="tpu_custom_call" | custom-call | flops 5000000000 | bytes 10000000 | tf_op jit(solution)/shard_map/block_0/pallas_call | solution.py:327
  190.7 16.0 %attention_0.1 = (bf16[4,512,128]{2,1,0:T(8,128)(2,1)}, f32[4,512,256]{2,1,0:T(8,128)}, bf16[4,512,256]{2,1,0:T(8,128)(2,1)}) custom-call(f32[1]{0:T(128)} %bitcast.1.refs_0_.bias, bf16[4,512,128]{2,1,0:T(8,128)(2,1)} %get-tuple-element.70.refs_1_.query, bf16[4,512,256]{2,1,0:T(8,128)(2,1)} %get-tuple-element.71.refs_2_.pair, ...), custom_call_target="tpu_custom_call" | custom-call | flops 5000000000 | bytes 10000000 | tf_op jit(solution)/shard_map/attention_0/pallas_call | solution.py:327
  206.9 2.9 pad_maximum_fusion.4
  216.5 2.2 collective-permute-done.31
  219.8 8.1 %input_0.1 = (bf16[4,512,384]{2,1,0:T(8,128)(2,1)}, f32[512,512]{1,0:T(8,128)}, f32[4,8,128]{2,1,0:T(8,128)}, f32[4,8,128]{2,1,0:T(8,128)}) custom-call(bf16[4,512,128]{2,1,0:T(8,128)(2,1)} %get-tuple-element.104.query_grad, f32[4,512,256]{2,1,0:T(8,128)} %get-tuple-element.105.here, bf16[4,512,256]{2,1,0:T(8,128)(2,1)} %copy-done.24, ...), custom_call_target="tpu_custom_call" | custom-call | flops 2000000000 | bytes 10000000 | tf_op jit(solution)/shard_map/input_0/pallas_call | solution.py:327
  229.5 2.6 pad_maximum_fusion.5
  234.3 2.2 add_convert_fusion.1
  239.2 2.2 add_convert_fusion
  247.5 16.4 %collective-permute-done.27 = bf16[2,512,512]{2,1,0:T(8,128)(2,1)} collective-permute-done((bf16[2,512,512]{2,1,0:T(8,128)(2,1)}, bf16[2,512,512]{2,1,0:T(8,128)(2,1)}, u32[]{:S(2)}, u32[]{:S(2)}) %collective-permute-start.27) | collective-permute-done | bytes 1048608 | tf_op jit(solution)/shard_map/ppermute | solution.py:357
  265.5 20.9 %collective-permute-done.29 = bf16[2,512,512]{2,1,0:T(8,128)(2,1)} collective-permute-done((bf16[2,512,512]{2,1,0:T(8,128)(2,1)}, bf16[2,512,512]{2,1,0:T(8,128)(2,1)}, u32[]{:S(2)}, u32[]{:S(2)}) %collective-permute-start.29) | collective-permute-done | bytes 1048608 | tf_op jit(solution)/shard_map/ppermute | solution.py:357
  288.0 13.9 %collective-permute-done.33 = bf16[2,512,384]{2,1,0:T(8,128)(2,1)S(1)} collective-permute-done((bf16[2,512,384]{2,1,0:T(8,128)(2,1)S(1)}, bf16[2,512,384]{2,1,0:T(8,128)(2,1)S(1)}, u32[]{:S(2)}, u32[]{:S(2)}) %collective-permute-start.33) | collective-permute-done | bytes 786464 | tf_op jit(solution)/shard_map/ppermute | solution.py:357
  303.0 2.4 reshape.133
  312.6 50.4 %psum.15 = f32[2,8,512]{2,1,0:T(8,128)S(1)} all-reduce(f32[2,8,512]{2,1,0:T(8,128)S(1)} %pad_maximum_fusion.8), channel_id=1, replica_groups=mesh['wide'=16,'narrow'=2] {'wide','narrow'}, use_global_device_ids=true, to_apply=%region_1.2 | all-reduce | flops 8192 | bytes 65536 | tf_op jit(solution)/shard_map/psum | solution.py:497
  367.7 72.1 %all-reduce.2.cloned.1.call-done = bf16[3075,512]{1,0:T(8,128)(2,1)} async-done(((bf16[3075,512]{1,0:T(8,128)(2,1)}), bf16[3075,512]{1,0:T(8,128)(2,1)}) %all-reduce.2.cloned.1.call-update) | async-done | bytes 3148816 | tf_op jit(solution)/shard_map/psum | solution.py:491
  442.9 3.2 fusion.10
  453.1 2.2 pad_maximum_fusion.2
  455.3 2.4 copy.84
  459.8 2.5 pad_maximum_fusion.1
  464.3 2.4 pad_maximum_fusion
  (266 shorter events, 97.6 us)
Async XLA Ops:
  7.2 432.6 %all-reduce.2.cloned.1.call-start = ((), (), s32[]{:S(2)}) async-start(), calls=%async_computation | async-start | bytes 6307840 | tf_op jit(solution)/shard_map/psum | solution.py:491
  8.5 45.7 %collective-permute-start = (f32[8,128]{1,0:T(8,128)}, f32[8,128]{1,0:T(8,128)}, u32[]{:S(2)}, u32[]{:S(2)}) collective-permute-start(f32[8,128]{1,0:T(8,128)} %broadcast_in_dim.2), channel_id=1, source_target_pairs={{0,0},{1,2},{2,1},{3,3},{4,4},{5,6},{6,5},{7,7},{8,8},{9,10},{10,9... | collective-permute-start | bytes 12296 | tf_op jit(solution)/shard_map/ppermute | solution.py:357
  11.1 28.0 %collective-permute-start.4 = (f32[2,1536]{1,0:T(2,128)S(1)}, f32[2,1536]{1,0:T(2,128)}, u32[]{:S(2)}, u32[]{:S(2)}) collective-permute-start(f32[2,1536]{1,0:T(2,128)S(1)} %pad_maximum_fusion.9), channel_id=1, source_target_pairs={{0,1},{1,0},{2,3},{3,2},{4,5},{5,4},{6,7},{7,6},{8,9},{9,8},{10,11... | collective-permute-start | bytes 36872 | tf_op jit(solution)/shard_map/ppermute | solution.py:357
  14.1 28.8 %collective-permute-start.1 = (bf16[512,512]{1,0:T(8,128)(2,1)}, bf16[512,512]{1,0:T(8,128)(2,1)}, u32[]{:S(2)}, u32[]{:S(2)}) collective-permute-start(bf16[512,512]{1,0:T(8,128)(2,1)} %param.17), channel_id=1, source_target_pairs={{0,0},{1,2},{2,1},{3,3},{4,4},{5,6},{6,5},{7,7},{8,8},{9,10},{10,9... | collective-permute-start | bytes 1572872 | tf_op jit(solution)/shard_map/ppermute | solution.py:357
  21.7 18.9 %collective-permute-start.2 = (bf16[512,384]{1,0:T(8,128)(2,1)S(1)}, bf16[512,384]{1,0:T(8,128)(2,1)}, u32[]{:S(2)}, u32[]{:S(2)}) collective-permute-start(bf16[512,384]{1,0:T(8,128)(2,1)S(1)} %bitcast.182), channel_id=1, source_target_pairs={{0,1},{1,0},{2,3},{3,2},{4,5},{5,4},{6,7},{7,6},{8,9},{9,8},{10,11... | collective-permute-start | bytes 1179656 | tf_op jit(solution)/shard_map/ppermute | solution.py:357
  22.7 42.8 %collective-permute-start.12 = (bf16[512,384]{1,0:T(8,128)(2,1)}, bf16[512,384]{1,0:T(8,128)(2,1)}, u32[]{:S(2)}, u32[]{:S(2)}) collective-permute-start(bf16[512,384]{1,0:T(8,128)(2,1)} %bitcast.23), channel_id=1, source_target_pairs={{0,1},{1,0},{2,3},{3,2},{4,5},{5,4},{6,7},{7,6},{8,9},{9,8},{10,11... | collective-permute-start | bytes 1179656 | tf_op jit(solution)/shard_map/ppermute | solution.py:357
  39.1 18.4 %collective-permute-start.10 = (bf16[512,512]{1,0:T(8,128)(2,1)}, bf16[512,512]{1,0:T(8,128)(2,1)}, u32[]{:S(2)}, u32[]{:S(2)}) collective-permute-start(bf16[512,512]{1,0:T(8,128)(2,1)} %dynamic-slice_bitcast_fusion.2), channel_id=1, source_target_pairs={{0,1},{1,0},{2,3},{3,2},{4,5},{5,4},{6,7},{7,6},{8,9},{9,8},{10,11... | collective-permute-start | bytes 1572872 | tf_op jit(solution)/shard_map/ppermute | solution.py:357
  42.9 22.7 %collective-permute-start.8 = (bf16[512,512]{1,0:T(8,128)(2,1)}, bf16[512,512]{1,0:T(8,128)(2,1)}, u32[]{:S(2)}, u32[]{:S(2)}) collective-permute-start(bf16[512,512]{1,0:T(8,128)(2,1)} %dynamic-slice_bitcast_fusion.3), channel_id=1, source_target_pairs={{0,1},{1,0},{2,3},{3,2},{4,5},{5,4},{6,7},{7,6},{8,9},{9,8},{10,11... | collective-permute-start | bytes 1572872 | tf_op jit(solution)/shard_map/ppermute | solution.py:357
  50.1 22.0 %collective-permute-start.5 = (bf16[4,512,256]{2,1,0:T(8,128)(2,1)}, bf16[4,512,256]{2,1,0:T(8,128)(2,1)}, u32[]{:S(2)}, u32[]{:S(2)}) collective-permute-start(bf16[4,512,256]{2,1,0:T(8,128)(2,1)} %get-tuple-element.71.refs_2_.pair), channel_id=1, source_target_pairs={{0,2},{1,3},{2,0},{3,1},{4,6},{5,7},{6,4},{7,5},{8,10},{9,11},{10,... | collective-permute-start | bytes 3145736 | tf_op jit(solution)/shard_map/ppermute | solution.py:357
  54.2 13.1 %collective-permute-start.6 = (bf16[128,512]{1,0:T(8,128)(2,1)S(1)}, bf16[128,512]{1,0:T(8,128)(2,1)S(1)}, u32[]{:S(2)}, u32[]{:S(2)}) collective-permute-start(bf16[128,512]{1,0:T(8,128)(2,1)S(1)} %dynamic-slice_bitcast_fusion.5), channel_id=1, source_target_pairs={{0,1},{1,0},{2,3},{3,2},{4,5},{5,4},{6,7},{7,6},{8,9},{9,8},{10,11... | collective-permute-start | bytes 393224 | tf_op jit(solution)/shard_map/ppermute | solution.py:357
  57.5 14.6 %collective-permute-start.11 = (bf16[512,512]{1,0:T(8,128)(2,1)}, bf16[512,512]{1,0:T(8,128)(2,1)S(1)}, u32[]{:S(2)}, u32[]{:S(2)}) collective-permute-start(bf16[512,512]{1,0:T(8,128)(2,1)} %collective-permute-done.10.refs_12_.refs_17_), channel_id=1, source_target_pairs={{0,2},{1,3},{2,0},{3,1},{4,6},{5,7},{6,4},{7,5},{8,10},{9,11},{10,... | collective-permute-start | bytes 1572872 | tf_op jit(solution)/shard_map/ppermute | solution.py:357
  70.0 26.8 %collective-permute-start.19 = (bf16[512,512]{1,0:T(8,128)(2,1)S(1)}, bf16[512,512]{1,0:T(8,128)(2,1)}, u32[]{:S(2)}, u32[]{:S(2)}) collective-permute-start(bf16[512,512]{1,0:T(8,128)(2,1)S(1)} %copy-done.18), channel_id=1, source_target_pairs={{0,1},{1,0},{2,3},{3,2},{4,5},{5,4},{6,7},{7,6},{8,9},{9,8},{10,11... | collective-permute-start | bytes 1572872 | tf_op jit(solution)/shard_map/ppermute | solution.py:357
  70.9 26.4 %collective-permute-start.17 = (bf16[512,512]{1,0:T(8,128)(2,1)S(1)}, bf16[512,512]{1,0:T(8,128)(2,1)}, u32[]{:S(2)}, u32[]{:S(2)}) collective-permute-start(bf16[512,512]{1,0:T(8,128)(2,1)S(1)} %dynamic-slice_bitcast_fusion.1), channel_id=1, source_target_pairs={{0,1},{1,0},{2,3},{3,2},{4,5},{5,4},{6,7},{7,6},{8,9},{9,8},{10,11... | collective-permute-start | bytes 1572872 | tf_op jit(solution)/shard_map/ppermute | solution.py:357
  96.8 8.0 %collective-permute-start.14 = (bf16[4,512,256]{2,1,0:T(8,128)(2,1)}, bf16[4,512,256]{2,1,0:T(8,128)(2,1)S(1)}, u32[]{:S(2)}, u32[]{:S(2)}) collective-permute-start(bf16[4,512,256]{2,1,0:T(8,128)(2,1)} %get-tuple-element.73.refs_2_.pair), channel_id=1, source_target_pairs={{0,2},{1,3},{2,0},{3,1},{4,6},{5,7},{6,4},{7,5},{8,10},{9,11},{10,... | collective-permute-start | bytes 3145736 | tf_op jit(solution)/shard_map/ppermute | solution.py:357
  96.9 7.8 %collective-permute-start.20 = (bf16[512,512]{1,0:T(8,128)(2,1)}, bf16[512,512]{1,0:T(8,128)(2,1)S(1)}, u32[]{:S(2)}, u32[]{:S(2)}) collective-permute-start(bf16[512,512]{1,0:T(8,128)(2,1)} %collective-permute-done.19.refs_12_.refs_17_), channel_id=1, source_target_pairs={{0,2},{1,3},{2,0},{3,1},{4,6},{5,7},{6,4},{7,5},{8,10},{9,11},{10,... | collective-permute-start | bytes 1572872 | tf_op jit(solution)/shard_map/ppermute | solution.py:357
  97.4 7.4 %collective-permute-start.18 = (bf16[512,512]{1,0:T(8,128)(2,1)}, bf16[512,512]{1,0:T(8,128)(2,1)S(1)}, u32[]{:S(2)}, u32[]{:S(2)}) collective-permute-start(bf16[512,512]{1,0:T(8,128)(2,1)} %collective-permute-done.17.refs_9_.refs_14_), channel_id=1, source_target_pairs={{0,2},{1,3},{2,0},{3,1},{4,6},{5,7},{6,4},{7,5},{8,10},{9,11},{10,... | collective-permute-start | bytes 1572872 | tf_op jit(solution)/shard_map/ppermute | solution.py:357
  103.4 23.3 %collective-permute-start.22 = (bf16[512,512]{1,0:T(8,128)(2,1)S(1)}, bf16[512,512]{1,0:T(8,128)(2,1)S(1)}, u32[]{:S(2)}, u32[]{:S(2)}) collective-permute-start(bf16[512,512]{1,0:T(8,128)(2,1)S(1)} %copy-done.26), channel_id=1, source_target_pairs={{0,0},{1,2},{2,1},{3,3},{4,4},{5,6},{6,5},{7,7},{8,8},{9,10},{10,9... | collective-permute-start | bytes 1572872 | tf_op jit(solution)/shard_map/ppermute | solution.py:357
  190.3 19.9 %collective-permute-start.30 = (bf16[2,2,128,512]{3,2,0,1:T(8,128)(2,1)S(1)}, bf16[2,2,128,512]{3,2,0,1:T(8,128)(2,1)S(1)}, u32[]{:S(2)}, u32[]{:S(2)}) collective-permute-start(bf16[2,2,128,512]{3,2,0,1:T(8,128)(2,1)S(1)} %pad_maximum_fusion.7), channel_id=1, source_target_pairs={{0,2},{1,3},{2,0},{3,1},{4,6},{5,7},{6,4},{7,5},{8,10},{9,11},{10,... | collective-permute-start | bytes 1572872 | tf_op jit(solution)/shard_map/ppermute | solution.py:357
  206.7 12.1 %collective-permute-start.24 = (bf16[4,512,256]{2,1,0:T(8,128)(2,1)}, bf16[4,512,256]{2,1,0:T(8,128)(2,1)S(1)}, u32[]{:S(2)}, u32[]{:S(2)}) collective-permute-start(bf16[4,512,256]{2,1,0:T(8,128)(2,1)} %get-tuple-element.106), channel_id=1, source_target_pairs={{0,2},{1,3},{2,0},{3,1},{4,6},{5,7},{6,4},{7,5},{8,10},{9,11},{10,... | collective-permute-start | bytes 3145736 | tf_op jit(solution)/shard_map/ppermute | solution.py:357
  209.8 24.5 %collective-permute-start.26 = (bf16[2,2,512,512]{3,2,0,1:T(8,128)(2,1)}, bf16[2,2,512,512]{3,2,0,1:T(8,128)(2,1)}, u32[]{:S(2)}, u32[]{:S(2)}) collective-permute-start(bf16[2,2,512,512]{3,2,0,1:T(8,128)(2,1)} %pad_maximum_fusion.4), channel_id=1, source_target_pairs={{0,2},{1,3},{2,0},{3,1},{4,6},{5,7},{6,4},{7,5},{8,10},{9,11},{10,... | collective-permute-start | bytes 6291464 | tf_op jit(solution)/shard_map/ppermute | solution.py:357
  210.3 8.4 %collective-permute-start.31 = (bf16[2,128,512]{2,1,0:T(8,128)(2,1)S(1)}, bf16[2,128,512]{2,1,0:T(8,128)(2,1)S(1)}, u32[]{:S(2)}, u32[]{:S(2)}) collective-permute-start(bf16[2,128,512]{2,1,0:T(8,128)(2,1)S(1)} %slice_bitcast_fusion.6), channel_id=1, source_target_pairs={{0,1},{1,0},{2,3},{3,2},{4,5},{5,4},{6,7},{7,6},{8,9},{9,8},{10,11... | collective-permute-start | bytes 786440 | tf_op jit(solution)/shard_map/ppermute | solution.py:357
  213.2 24.7 %collective-permute-start.28 = (bf16[2,2,512,512]{3,2,0,1:T(8,128)(2,1)}, bf16[2,2,512,512]{3,2,0,1:T(8,128)(2,1)}, u32[]{:S(2)}, u32[]{:S(2)}) collective-permute-start(bf16[2,2,512,512]{3,2,0,1:T(8,128)(2,1)} %pad_maximum_fusion.3), channel_id=1, source_target_pairs={{0,2},{1,3},{2,0},{3,1},{4,6},{5,7},{6,4},{7,5},{8,10},{9,11},{10,... | collective-permute-start | bytes 6291464 | tf_op jit(solution)/shard_map/ppermute | solution.py:357
  232.1 11.4 %collective-permute-start.32 = (bf16[2,2,512,384]{3,2,0,1:T(8,128)(2,1)}, bf16[2,2,512,384]{3,2,0,1:T(8,128)(2,1)}, u32[]{:S(2)}, u32[]{:S(2)}) collective-permute-start(bf16[2,2,512,384]{3,2,0,1:T(8,128)(2,1)} %pad_maximum_fusion.5), channel_id=1, source_target_pairs={{0,2},{1,3},{2,0},{3,1},{4,6},{5,7},{6,4},{7,5},{8,10},{9,11},{10,... | collective-permute-start | bytes 4718600 | tf_op jit(solution)/shard_map/ppermute | solution.py:357
  232.6 10.9 %collective-permute-start.35 = (bf16[2,768]{1,0:T(2,128)(2,1)S(1)}, bf16[2,768]{1,0:T(2,128)(2,1)S(1)}, u32[]{:S(2)}, u32[]{:S(2)}) collective-permute-start(bf16[2,768]{1,0:T(2,128)(2,1)S(1)} %bitcast.203), channel_id=1, source_target_pairs={{0,1},{1,0},{2,3},{3,2},{4,5},{5,4},{6,7},{7,6},{8,9},{9,8},{10,11... | collective-permute-start | bytes 9224 | tf_op jit(solution)/shard_map/ppermute | solution.py:357
  237.5 26.3 %collective-permute-start.27 = (bf16[2,512,512]{2,1,0:T(8,128)(2,1)}, bf16[2,512,512]{2,1,0:T(8,128)(2,1)}, u32[]{:S(2)}, u32[]{:S(2)}) collective-permute-start(bf16[2,512,512]{2,1,0:T(8,128)(2,1)} %slice_bitcast_fusion.2), channel_id=1, source_target_pairs={{0,1},{1,0},{2,3},{3,2},{4,5},{5,4},{6,7},{7,6},{8,9},{9,8},{10,11... | collective-permute-start | bytes 3145736 | tf_op jit(solution)/shard_map/ppermute | solution.py:357
  243.1 43.3 %collective-permute-start.29 = (bf16[2,512,512]{2,1,0:T(8,128)(2,1)}, bf16[2,512,512]{2,1,0:T(8,128)(2,1)}, u32[]{:S(2)}, u32[]{:S(2)}) collective-permute-start(bf16[2,512,512]{2,1,0:T(8,128)(2,1)} %slice_bitcast_fusion), channel_id=1, source_target_pairs={{0,1},{1,0},{2,3},{3,2},{4,5},{5,4},{6,7},{7,6},{8,9},{9,8},{10,11... | collective-permute-start | bytes 3145736 | tf_op jit(solution)/shard_map/ppermute | solution.py:357
  245.8 56.1 %collective-permute-start.33 = (bf16[2,512,384]{2,1,0:T(8,128)(2,1)S(1)}, bf16[2,512,384]{2,1,0:T(8,128)(2,1)S(1)}, u32[]{:S(2)}, u32[]{:S(2)}) collective-permute-start(bf16[2,512,384]{2,1,0:T(8,128)(2,1)S(1)} %slice_bitcast_fusion.4), channel_id=1, source_target_pairs={{0,1},{1,0},{2,3},{3,2},{4,5},{5,4},{6,7},{7,6},{8,9},{9,8},{10,11... | collective-permute-start | bytes 2359304 | tf_op jit(solution)/shard_map/ppermute | solution.py:357
  310.5 56.1 %collective-permute-start.25 = (bf16[512,512]{1,0:T(8,128)(2,1)S(1)}, bf16[512,512]{1,0:T(8,128)(2,1)S(1)}, u32[]{:S(2)}, u32[]{:S(2)}) collective-permute-start(bf16[512,512]{1,0:T(8,128)(2,1)S(1)} %convert_element_type.163), channel_id=1, source_target_pairs={{0,0},{1,2},{2,1},{3,3},{4,4},{5,6},{6,5},{7,7},{8,8},{9,10},{10,9... | collective-permute-start | bytes 1572872 | tf_op jit(solution)/shard_map/ppermute | solution.py:357
  441.6 6.8 %collective-permute-start.38 = (bf16[2,128,512]{2,1,0:T(8,128)(2,1)S(1)}, bf16[2,128,512]{2,1,0:T(8,128)(2,1)S(1)}, u32[]{:S(2)}, u32[]{:S(2)}) collective-permute-start(bf16[2,128,512]{2,1,0:T(8,128)(2,1)S(1)} %bitcast.174), channel_id=1, source_target_pairs={{0,2},{1,3},{2,0},{3,1},{4,6},{5,7},{6,4},{7,5},{8,10},{9,11},{10,... | collective-permute-start | bytes 786440 | tf_op jit(solution)/shard_map/ppermute | solution.py:357
  442.8 6.8 %collective-permute-start.36 = (bf16[2,512,384]{2,1,0:T(8,128)(2,1)S(1)}, bf16[2,512,384]{2,1,0:T(8,128)(2,1)S(1)}, u32[]{:S(2)}, u32[]{:S(2)}) collective-permute-start(bf16[2,512,384]{2,1,0:T(8,128)(2,1)S(1)} %reshape.135), channel_id=1, source_target_pairs={{0,2},{1,3},{2,0},{3,1},{4,6},{5,7},{6,4},{7,5},{8,10},{9,11},{10,... | collective-permute-start | bytes 2359304 | tf_op jit(solution)/shard_map/ppermute | solution.py:357
  446.1 16.1 %collective-permute-start.39 = (bf16[2,512,512]{2,1,0:T(8,128)(2,1)}, bf16[2,512,512]{2,1,0:T(8,128)(2,1)}, u32[]{:S(2)}, u32[]{:S(2)}) collective-permute-start(bf16[2,512,512]{2,1,0:T(8,128)(2,1)} %bitcast.59), channel_id=1, source_target_pairs={{0,2},{1,3},{2,0},{3,1},{4,6},{5,7},{6,4},{7,5},{8,10},{9,11},{10,... | collective-permute-start | bytes 3145736 | tf_op jit(solution)/shard_map/ppermute | solution.py:357
  446.4 11.2 %collective-permute-start.40 = (bf16[2,512,512]{2,1,0:T(8,128)(2,1)}, bf16[2,512,512]{2,1,0:T(8,128)(2,1)}, u32[]{:S(2)}, u32[]{:S(2)}) collective-permute-start(bf16[2,512,512]{2,1,0:T(8,128)(2,1)} %bitcast.60), channel_id=1, source_target_pairs={{0,2},{1,3},{2,0},{3,1},{4,6},{5,7},{6,4},{7,5},{8,10},{9,11},{10,... | collective-permute-start | bytes 3145736 | tf_op jit(solution)/shard_map/ppermute | solution.py:357
  (49 other events, 275.6 us)
Sparse Core Ops, SparseCore 0:
  308.4 131.3 all-reduce.1

commit v2 on v1

--- a/solution.py
+++ b/solution.py
@@ -174,6 +174,16 @@
         project(low_ref[...], wi, query_bias, value_bias, query_ref, pair_ref)
 
 
+def place_quarter(mine_ref, theirs_ref, index, at, size, value):
+    @pl.when(index < 2)
+    def _():
+        mine_ref[index, at : at + size] = value
+
+    @pl.when(index >= 2)
+    def _():
+        theirs_ref[index - 2, at : at + size] = value
+
+
 def column_sum(x):
     return jnp.sum(x, 0, keepdims=True)
 
@@ -187,7 +197,7 @@
 
 def block_kernel(layer, *refs):
     (grad, second, second_scale, active, slope, normed, first, first_scale, mixed, vectors, wo_own, wo_mine, wo_theirs, we_own, we_mine, we_theirs, ws_own, ws_mine, ws_theirs), refs = refs[:19], refs[19:]
-    (shrink_ref, expand_ref, output_ref, summed_ref, mixed_grad_ref, inner_ref, vector_ref, expand_bias_ref), refs = refs[:8], refs[8:]
+    (mine_ref, theirs_ref, summed_ref, mixed_grad_ref, inner_ref, vector_ref, expand_bias_ref), refs = refs[:7], refs[7:]
     wo, we, ws, acc, turned, sem = refs
     core = lax.rem(lax.axis_index("wide"), 2)
     units = we.shape[2]
@@ -199,6 +209,10 @@
     we_copies = start_quarters((columns(core), columns(1 - core)), we_mine, we_theirs, we, sem.at[1], core)
     wo_copies = start_quarters((wo_own.at[layer, core], wo_own.at[layer, 1 - core]), wo_mine, wo_theirs, wo, sem.at[0], core)
     rows, width = mixed.shape[1], mixed.shape[2]
+
+    def put(index, at, size, value):
+        place_quarter(mine_ref, theirs_ref, index, at, size, value)
+
     incoming = grad[...].astype(F32)
     widened = norm_backward(incoming, second[...], second_scale[...], vectors[4:5])
     vector_ref[0:1] = column_sum(incoming)
@@ -213,8 +227,8 @@
     def one_quarter(index, carry):
         active_grad = dot_rt(branch, ws[index])
         inner = (active_grad * slope[index].astype(F32)).astype(BF16)
-        shrink_ref[index] = dot_lt(active[index], branch).astype(BF16)
-        expand_ref[index] = dot(turned[...], inner).astype(BF16)
+        put(index, 0, units, dot_lt(active[index], branch).astype(BF16))
+        put(index, units, turned.shape[0], dot(turned[...], inner).astype(BF16))
         expand_bias_ref[index] = jnp.broadcast_to(column_sum(inner.astype(F32)), expand_bias_ref.shape[1:])
         acc[...] += dot_rt(inner, we[index])
         return carry
@@ -236,7 +250,7 @@
     def one_pair(index, carry):
         mixed_grad = dot_rt(low, wo[index]).astype(BF16)
         mixed_grad_ref[index] = mixed_grad
-        output_ref[index] = dot_lt(mixed[index], low).astype(BF16)
+        put(index, units + turned.shape[0], width, dot_lt(mixed[index], low).astype(BF16))
         product = mixed_grad.astype(F32) * mixed[index].astype(F32)
         inner_ref[index] = lax.dot_general(
             selector, product, (((1,), (1,)), ((), ())), precision=lax.Precision.HIGHEST, preferred_element_type=F32
@@ -288,10 +302,9 @@
     lax.fori_loop(0, 4, one_pair, 0)
 
 
-def input_kernel(query_grad, here, away, hidden_low, summed, wi_own, wi_mine, wi_theirs, weight_ref, grad_ref, query_bias_ref, value_bias_ref, wi, turned, acc, sem):
+def input_kernel(query_grad, here, away, hidden_low, summed, wi_own, wi_mine, wi_theirs, mine_ref, theirs_ref, grad_ref, triple_ref, wi, turned, acc, sem):
     core = lax.rem(lax.axis_index("wide"), 2)
     copies = start_quarters((wi_own.at[core], wi_own.at[1 - core]), wi_mine, wi_theirs, wi, sem, core)
-    width = query_grad.shape[2]
     turned[...] = hidden_low[...].T
     acc[...] = summed[...]
     finish(copies)
@@ -299,11 +312,9 @@
     def one(index, carry):
         pair_grad = (here[index] + away[index].astype(F32)).astype(BF16)
         triple = jnp.concatenate([query_grad[index], pair_grad], 1)
-        weight_ref[index] = dot(turned[...], triple).astype(BF16)
+        place_quarter(mine_ref, theirs_ref, index, 0, turned.shape[0], dot(turned[...], triple).astype(BF16))
         acc[...] += dot_rt(triple, wi[index])
-        sums = column_sum(triple.astype(F32))
-        query_bias_ref[index] = jnp.broadcast_to(sums[:, :width], query_bias_ref.shape[1:])
-        value_bias_ref[index] = jnp.broadcast_to(sums[:, 2 * width :], value_bias_ref.shape[1:])
+        triple_ref[index] = jnp.broadcast_to(column_sum(triple.astype(F32)), triple_ref.shape[1:])
         return carry
 
     lax.fori_loop(0, 4, one, 0)
@@ -446,85 +457,266 @@
     collected = [None] * layers
     for layer in reversed(range(layers)):
         low, query, pair, remote, mixed, total, normed, first, first_scale, active, slope, second, second_scale = saved[layer]
-        shrink_grad, expand_grad, output_grad, summed, mixed_grad, inner, vector_grad, expand_bias_grad = call(
+        mine, theirs, summed, mixed_grad, inner, vector_grad, expand_bias_grad = call(
             functools.partial(block_kernel, layer), f"block_{layer}",
             [VM] * 10 + [AN] * 9,
-            [shaped(BF16, 4, units, depth), shaped(BF16, 4, depth, units), shaped(BF16, 4, width, depth), row_shape, query_shape, stat_shape, shaped(F32, 8, depth), shaped(F32, 4, 8, units)],
+            [shaped(BF16, 2, units + depth + width, depth)] * 2 + [row_shape, query_shape, stat_shape, shaped(F32, 8, depth), shaped(F32, 4, 8, units)],
             [wo_scratch, we_scratch, ws_scratch, acc_scratch, turn_scratch, pltpu.SemaphoreType.DMA((3, 4))],
             (grad, second, second_scale, active, slope, normed, first, first_scale, mixed, vectors[layer], output_own, *fetched[layer][1], expand_weight, *fetched[layer][2], shrink_own, *fetched[layer][3]),
             5 * 10**9,
         )
+        blocks = reduce_quarters(mine, theirs, send, partner, across)
         query_grad, here, away = call(
             attention_kernel, f"attention_{layer}",
             [SM] + [VM] * 6, [query_shape, shaped(F32, 4, rows, 2 * width), pair_shape], [],
             (shift, query, pair, remote, mixed_grad, total, inner), 5 * 10**9,
         )
         back = send(away, partner)
-        input_grad, grad, query_bias_grad, value_bias_grad = call(
+        mine, theirs, grad, triple_grad = call(
             input_kernel, f"input_{layer}",
             [VM] * 5 + [AN] * 3,
-            [shaped(BF16, 4, depth, 3 * width), row_shape, shaped(F32, 4, 8, width), shaped(F32, 4, 8, width)],
+            [shaped(BF16, 2, depth, 3 * width)] * 2 + [row_shape, shaped(F32, 4, 8, 3 * width)],
             [wi_scratch, turn_scratch, acc_scratch, pltpu.SemaphoreType.DMA((4,))],
             (query_grad, here, back, low, summed, input_own[layer], *fetched[layer][0]), 2 * 10**9,
         )
-        collected[layer] = (shrink_grad, expand_grad, output_grad, input_grad, vector_grad, expand_bias_grad, query_bias_grad, value_bias_grad)
+        collected[layer] = (blocks, mine, theirs, vector_grad, expand_bias_grad, triple_grad)
     input_rows = send(grad.astype(BF16), swap).astype(F32)
-    return reduce_all(collected, layer_output, input_rows, send, core, across, partner, wide, layers, depth, width, units)
-
-
-def reduce_all(collected, layer_output, input_rows, send, core, across, partner, wide, layers, depth, width, units):
-    names = list(zip(*collected))
-    shrink_grad, expand_grad, output_grad, input_grad = (jnp.stack(item, 1) for item in names[:4])
-    vector_grad = jnp.stack(names[4], 0)
-    narrow_rows = jnp.stack(
-        [jnp.concatenate([q[:, 0], v[:, 0], e[:, 0]], 1) for e, q, v in zip(names[5], names[6], names[7])], 1
-    )
+    return finish_all(collected, layer_output, input_rows, send, core, across, partner, wide, layers, depth, width, units)
+
+
+def reduce_quarters(mine, theirs, send, partner, across):
+    mine = (mine.astype(F32) + send(theirs, partner).astype(F32)).astype(BF16)
+    return (mine[0].astype(F32) + send(mine[1], across).astype(F32)).astype(BF16)
+
+
+def finish_all(collected, layer_output, input_rows, send, core, across, partner, wide, layers, depth, width, units):
     same = [[w for w in range(wide) if w % 2 == c] for c in range(2)]
-
-    def reduce_quarters(x):
-        mine = (x[:2].astype(F32) + send(x[2:], partner).astype(F32)).astype(BF16)
-        mine = (mine[0].astype(F32) + send(mine[1], across).astype(F32)).astype(BF16)
-        return mine
-
-    parts = [reduce_quarters(x) for x in (shrink_grad, expand_grad, output_grad, input_grad, narrow_rows.astype(BF16))]
-    flat = jnp.concatenate([p.reshape(-1, 512) for p in parts], 0)
-    flat = lax.psum(flat, "wide", axis_index_groups=same)
-    done, at = [], 0
-    for p in parts:
-        size = p.size // 512
-        done.append(flat[at : at + size].reshape(p.shape))
-        at += size
-    vector_grad = lax.psum(vector_grad, AXES)
-
-    def spread(x):
-        there = send(x, partner)
-        x, there = x.astype(F32), there.astype(F32)
-        return jnp.where(core == 0, x, there), jnp.where(core == 0, there, x)
-
-    shrink_one, shrink_two = spread(done[0])
-    expand_one, expand_two = spread(done[1])
-    output_one, output_two = spread(done[2])
-    input_one, input_two = spread(done[3])
-    rows_one, rows_two = spread(done[4])
-    triple = lambda x: x.reshape(layers, depth, 3, width)
-    columns = lambda a, b: jnp.concatenate([rows_one[:, a:b], rows_two[:, a:b]], 1)
+    smalls = []
+    for blocks, mine, theirs, vector_grad, expand_bias_grad, triple_grad in collected:
+        triple = jnp.pad(triple_grad[:, :1], ((0, 0), (0, 0), (0, depth - 3 * width)))
+        expand = jnp.pad(expand_bias_grad[:, :1], ((0, 0), (0, 0), (0, depth - units)))
+        smalls.append(jnp.concatenate([jnp.broadcast_to(vector_grad[:6], (4, 6, depth)), expand, triple], 1))
+    small = jnp.concatenate(smalls, 1)
+    done = []
+    for layer in range(1, layers):
+        blocks, mine, theirs = collected[layer][:3]
+        inputs = reduce_quarters(mine, theirs, send, partner, across)
+        blocks, inputs = lax.psum((blocks, inputs), "wide", axis_index_groups=same)
+        pair = []
+        for x in (blocks, inputs):
+            there = send(x, partner)
+            pair.append(jnp.where(core == 0, jnp.stack([x, there]), jnp.stack([there, x])))
+        done.append(pair)
+    blocks, mine, theirs = collected[0][:3]
+    blocks, inputs, small = finish_call(blocks, mine, theirs, small, wide)
+    done.insert(0, [blocks, inputs])
+    shrink, expand, output, inputs = [], [], [], []
+    for blocks, triple in done:
+        blocks, triple = blocks.astype(F32), triple.astype(F32)
+        shrink.append(blocks[:, :units].reshape(2 * units, depth))
+        expand.append(blocks[:, units : units + depth].transpose(1, 0, 2).reshape(depth, 2 * units))
+        output.append(blocks[:, units + depth : units + depth + width].reshape(2 * width, depth))
+        inputs.append(triple[:, :depth].reshape(2, depth, 3, width).transpose(1, 2, 0, 3).reshape(depth, 3, 2 * width))
+    small = small.reshape(2, layers, 8, depth)
+    both = lambda at, a, b: small[:, :, at, a:b].transpose(1, 0, 2).reshape(layers, 2 * (b - a))
+    vector = lambda at: small[0, :, at]
     return (
         layer_output,
         input_rows,
-        jnp.concatenate([triple(input_one), triple(input_two)], 3),
-        columns(0, width),
-        columns(width, 2 * width),
-        jnp.concatenate([output_one, output_two], 1),
-        vector_grad[:, 5],
-        vector_grad[:, 4],
-        vector_grad[:, 3],
-        jnp.concatenate([expand_one, expand_two], 2),
-        columns(2 * width, 2 * width + units),
-        jnp.concatenate([shrink_one, shrink_two], 1),
-        vector_grad[:, 2],
-        vector_grad[:, 1],
-        vector_grad[:, 0],
-    )
+        jnp.stack(inputs),
+        both(7, 0, width),
+        both(7, 2 * width, 3 * width),
+        jnp.stack(output),
+        vector(5),
+        vector(4),
+        vector(3),
+        jnp.stack(expand),
+        both(6, 0, units),
+        jnp.stack(shrink),
+        vector(2),
+        vector(1),
+        vector(0),
+    )
+
+
+def finish_kernel(chips, *refs):
+    (blocks, inputs_mine, inputs_theirs, small), refs = refs[:4], refs[4:]
+    (blocks_out, inputs_out, small_out), refs = refs[:3], refs[3:]
+    (held, held_inputs, *landed), refs = refs[:6], refs[6:]
+    (core_inputs, mid_inputs, row_inputs, core_small, mid_small, row_small, sum_small, step_small), refs = refs[:8], refs[8:]
+    ring_send, ring_recv, pair_send, pair_recv, step_send, step_recv = refs
+    wide, narrow = lax.axis_index("wide"), lax.axis_index("narrow")
+    core, chip = lax.rem(wide, 2), wide // 2
+    odd = lax.rem(chip, 2)
+    place = odd * (chips - 1 - chip // 2) + (1 - odd) * (chip // 2)
+
+    def chip_at(position):
+        position = lax.rem(position + chips, chips)
+        late = position // (chips // 2)
+        return late * (2 * (chips - 1 - position) + 1) + (1 - late) * (2 * position)
+
+    def peer(index, other_core=0, other_narrow=0):
+        side = core + other_core * (1 - 2 * core)
+        return (index * 2 + side, narrow + other_narrow * (1 - 2 * narrow))
+
+    right, left = peer(chip_at(place + 1)), peer(chip_at(place - 1))
+    beside, across = peer(chip, 1, 0), peer(chip, 0, 1)
+    steps = chips.bit_length() - 1
+    bits = []
+    for bit in range(steps):
+        flag = lax.rem(chip // 2**bit, 2)
+        bits.append(peer(chip + 2**bit * (1 - 2 * flag)))
+    barrier = pltpu.get_barrier_semaphore()
+    partners = [right, left, beside, across] + bits
+    for device in partners:
+        pl.semaphore_signal(barrier, inc=1, device_id=device, device_id_type=pl.DeviceIdType.MESH)
+    pl.semaphore_wait(barrier, len(partners))
+
+    sent = []
+
+    def remote(source, target, send_sem, recv_sem, device):
+        copy = pltpu.make_async_remote_copy(source, target, send_sem, recv_sem, device_id=device, device_id_type=pl.DeviceIdType.MESH)
+        copy.start()
+        sent.append(copy)
+        return copy
+
+    class Ring:
+        def __init__(self, which, data, out, columns, slots):
+            self.which, self.data, self.out, self.columns, self.slots = which, data, out, columns, slots
+            self.size = data.shape[0] // chips
+            self.now = [None, None]
+
+        def rows(self, index):
+            index = lax.rem(index + 2 * chips, chips)
+            return pl.ds(pl.multiple_of(index * self.size, 16), self.size)
+
+        def span(self, side):
+            at, count = self.columns[side]
+            return pl.ds(at, count)
+
+        def start(self):
+            for side in range(2):
+                self.pass_on(side, 0, self.data.at[self.rows(place), self.span(side)], self.slots[side].at[0])
+
+        def pass_on(self, side, step, source, target):
+            self.now[side] = remote(source, target, ring_send.at[self.which, side, step], ring_recv.at[self.which, side, step], (right, left)[side])
+
+        def tick(self, step):
+            for side in range(2):
+                way = 1 - 2 * side
+                span = self.span(side)
+                self.now[side].wait_recv()
+                if step < chips - 1:
+                    rows = self.rows(place - way * (step + 1))
+                    total = self.data[rows, span].astype(F32) + self.slots[side][step].astype(F32)
+                    total = total.astype(BF16)
+                    self.data[rows, span] = total
+                    if step < chips - 2:
+                        self.pass_on(side, step + 1, self.data.at[rows, span], self.slots[side].at[step + 1])
+                    else:
+                        self.out[core, rows, span] = total
+                        self.pass_on(side, step + 1, self.data.at[rows, span], self.out.at[core, rows, span])
+                elif step < 2 * chips - 3:
+                    rows = self.rows(place - way * (step - chips + 1))
+                    where = self.out.at[core, rows, span]
+                    self.pass_on(side, step + 1, where, where)
+
+    def fill(target, value):
+        target[0 : value.shape[0]] = value
+        if value.shape[0] < target.shape[0]:
+            target[value.shape[0] :] = jnp.zeros((target.shape[0] - value.shape[0], target.shape[1]), target.dtype)
+
+    fill(held, blocks[...])
+    half = held.shape[1] // 2
+    first = Ring(0, held, blocks_out, ((0, half), (half, half)), landed[0:2])
+    third = held_inputs.shape[1] // 3
+    second = Ring(1, held_inputs, inputs_out, ((0, 2 * third), (2 * third, third)), landed[2:4])
+    first.start()
+    copy_inputs = remote(inputs_theirs, core_inputs, pair_send.at[0], pair_recv.at[0], beside)
+    copy_small = remote(small.at[pl.ds(2, 2)], core_small, pair_send.at[1], pair_recv.at[1], beside)
+    copy_small.wait_recv()
+    mid_small[...] = small[1] + core_small[1]
+    copy_small = remote(mid_small, row_small, pair_send.at[2], pair_recv.at[2], across)
+    copy_inputs.wait_recv()
+    mid_inputs[...] = (inputs_mine[1].astype(F32) + core_inputs[1].astype(F32)).astype(BF16)
+    copy_inputs = remote(mid_inputs, row_inputs, pair_send.at[3], pair_recv.at[3], across)
+    fill(held_inputs, (inputs_mine[0].astype(F32) + core_inputs[0].astype(F32)).astype(BF16))
+    ticks = 2 * (chips - 1)
+    delay = 3
+    small_value = None
+    for step in range(ticks + delay):
+        if step < ticks:
+            first.tick(step)
+        if step == 0:
+            copy_small.wait_recv()
+            small_value = small[0] + core_small[0] + row_small[...]
+        if 0 < step <= steps:
+            copy_small.wait_recv()
+            small_value = small_value + step_small[step - 1]
+        if step < steps:
+            sum_small[step] = small_value
+            copy_small = remote(sum_small.at[step], step_small.at[step], step_send.at[step], step_recv.at[step], bits[step])
+        if step == steps:
+            small_out[core] = small_value
+        if step == delay - 1:
+            copy_inputs.wait_recv()
+            total = held_inputs[0 : row_inputs.shape[0]].astype(F32) + row_inputs[...].astype(F32)
+            held_inputs[0 : row_inputs.shape[0]] = total.astype(BF16)
+            second.start()
+        if step >= delay:
+            second.tick(step - delay)
+        if step == ticks:
+            last = [
+                remote(blocks_out.at[core], blocks_out.at[core], pair_send.at[4], pair_recv.at[4], beside),
+                remote(small_out.at[core], small_out.at[core], pair_send.at[5], pair_recv.at[5], beside),
+            ]
+    last.append(remote(inputs_out.at[core], inputs_out.at[core], pair_send.at[6], pair_recv.at[6], beside))
+    for copy in last:
+        copy.wait_recv()
+    for copy in sent:
+        copy.wait_send()
+
+
+def finish_call(blocks, inputs_mine, inputs_theirs, small, wide):
+    chips = wide // 2
+    size = lambda rows: -(-rows // (16 * chips)) * 16 * chips
+    rows, depth = blocks.shape
+    input_rows, columns = inputs_mine.shape[1:]
+    tall, input_tall = size(rows), size(input_rows)
+    steps = chips.bit_length() - 1
+    slot = lambda tall, count: pltpu.VMEM((chips - 1, tall // chips, count), BF16)
+    small_rows = small.shape[1]
+    return pl.pallas_call(
+        functools.partial(finish_kernel, chips),
+        out_shape=[shaped(BF16, 2, tall, depth), shaped(BF16, 2, input_tall, columns), shaped(F32, 2, small_rows, depth)],
+        in_specs=[VM] * 4,
+        out_specs=[VM] * 3,
+        scratch_shapes=[
+            pltpu.VMEM((tall, depth), BF16),
+            pltpu.VMEM((input_tall, columns), BF16),
+            slot(tall, depth // 2),
+            slot(tall, depth // 2),
+            slot(input_tall, 2 * columns // 3),
+            slot(input_tall, columns // 3),
+            pltpu.VMEM((2, input_rows, columns), BF16),
+            pltpu.VMEM((input_rows, columns), BF16),
+            pltpu.VMEM((input_rows, columns), BF16),
+            pltpu.VMEM((2, small_rows, depth), F32),
+            pltpu.VMEM((small_rows, depth), F32),
+            pltpu.VMEM((small_rows, depth), F32),
+            pltpu.VMEM((steps, small_rows, depth), F32),
+            pltpu.VMEM((steps, small_rows, depth), F32),
+            pltpu.SemaphoreType.DMA((2, 2, 2 * (chips - 1))),
+            pltpu.SemaphoreType.DMA((2, 2, 2 * (chips - 1))),
+            pltpu.SemaphoreType.DMA((7,)),
+            pltpu.SemaphoreType.DMA((7,)),
+            pltpu.SemaphoreType.DMA((steps,)),
+            pltpu.SemaphoreType.DMA((steps,)),
+        ],
+        compiler_params=pltpu.CompilerParams(collective_id=0, has_side_effects=True, vmem_limit_bytes=48 * 2**20),
+        cost_estimate=cost(10**9, 10**7),
+        name="finish",
+    )(blocks, inputs_mine, inputs_theirs, small)
 
 
 def solution(mesh):

time: 483 us -> 463 us (0.959)
  Pallas kernels: 130 us -> 202 us
  blocking collectives: 50.4 us -> 0 us
  waiting for transfers between devices: 142 us -> 110 us
  other arithmetic: 40.6 us -> 32.5 us
    pallas_call x0 -> x1, Pallas kernels: none -> 65.1 us  [finish_call(): pl.pallas_call(functools.partial(finish_kernel, chips), out_shape=[shaped...]
    psum x1 -> x0, blocking collectives: 50.4 us -> none  [reduce_all(): vector_grad = lax.psum(vector_grad, AXES)]
    ppermute x41 -> x34, waiting for transfers between devices: 70.4 us -> 46 us  [local(): send = lambda x, pairs: lax.ppermute(x, AXES, pairs)]
    concatenate x7 -> x0, other arithmetic: 9.88 us -> none  [the longest x1 2.46 us: reduce_all(): jnp.concatenate([shrink_one, shrink_two], 1)]
    psum x1, waiting for transfers between devices: 72.1 us -> 64.3 us  [finish_all(): blocks, inputs = lax.psum((blocks, inputs), 'wide', axis_index_groups=same)]
    transpose x0 -> x5, local copies, waits for them, and re-layouts: none -> 7.68 us  [the longest x3 6.7 us: finish_all(): blocks[:, units:units + depth].transpose(1, 0, 2).reshape(depth, 2 * units)]
    pallas_call x9, Pallas kernels: 130 us -> 137 us  [call(): pl.pallas_call(body, out_shape=outs, in_specs=ins, out_specs=[VM] * len(o...]
    ppermute x41 -> x34, starting transfers between devices: 32.6 us -> 27.8 us  [local(): send = lambda x, pairs: lax.ppermute(x, AXES, pairs)]
  transfers between devices with their start and end apart: 42 -> 35, of which waited for: 10 -> 8; matrix products, arithmetic and copies ran while one was open for 17% -> 14% of each run, Pallas kernels for 16% -> 37%
where the time goes in v2:
time: 463 us; the launch traced here: 454 us
  Pallas kernels  202 us (44%)
  waiting for transfers between devices  110 us (24%)
  local copies, waits for them, and re-layouts  65.1 us (14%)
  other arithmetic  32.5 us (7%)
  starting transfers between devices  27.8 us (6%)
  between operations  16.4 us (4%)
    pallas_call x9, Pallas kernels, call(): pl.pallas_call(body, out_shape=outs, in_specs=ins, out_specs=[VM] * len(o...  137 us
    pallas_call x1, Pallas kernels, finish_call(): pl.pallas_call(functools.partial(finish_kernel, chips), out_shape=[shaped...  65.1 us
    psum x1, waiting for transfers between devices, finish_all(): blocks, inputs = lax.psum((blocks, inputs), 'wide', axis_index_groups=same)  64.3 us
    ppermute x34, waiting for transfers between devices, local(): send = lambda x, pairs: lax.ppermute(x, AXES, pairs)  46 us
    ppermute x34, starting transfers between devices, local(): send = lambda x, pairs: lax.ppermute(x, AXES, pairs)  27.8 us
    unnamed x75, local copies, waits for them, and re-layouts  22.8 us
  transfers between devices with their start and end apart: 35, of which 8 were waited for; matrix products, arithmetic and copies ran while one was open for 14% of the time, Pallas kernels for 37%

profile of v2, /device:TPU:0, one launch (start us, length us, event | category | flops | bytes accessed | tf_op | source)
XLA Modules:
  0.0 454.1 jit_solution(12564931737760903287)
XLA Ops:
  11.1 3.0 collective-permute-start.4
  14.1 5.4 %collective-permute-start.1 = (bf16[512,512]{1,0:T(8,128)(2,1)}, bf16[512,512]{1,0:T(8,128)(2,1)}, u32[]{:S(2)}, u32[]{:S(2)}) collective-permute-start(bf16[512,512]{1,0:T(8,128)(2,1)} %param.17), channel_id=1, source_target_pairs={{0,0},{1,2},{2,1},{3,3},{4,4},{5,6},{6,5},{7,7},{8,8},{9,10},{10,9... | collective-permute-start | bytes 1572872 | tf_op jit(solution)/shard_map/ppermute | solution.py:368
  22.7 2.0 collective-permute-start.12
  25.8 2.8 fusion.6
  44.7 5.4 %first.1 = (bf16[4,512,128]{2,1,0:T(8,128)(2,1)}, bf16[4,512,256]{2,1,0:T(8,128)(2,1)}) custom-call(bf16[512,512]{1,0:T(8,128)(2,1)} %collective-permute-done.1.tokens.hidden_low, bf16[2,512,384]{2,1,0:T(8,128)(2,1)} %copy.83.weight_own.wi_own, bf16[512,384]{1,0:T(8,128)(2,1)} %collective-permute-done.2.weight_mine.wi_mine, bf16[512,384]{1,0:T(8,128)(2,1)} %copy-done.26, ...), custom_call_target="tpu_custom_call" | custom-call | flops 1000000000 | bytes 10000000 | tf_op jit(solution)/shard_map/first/pallas_call | solution.py:338
  57.9 7.7 %collective-permute-done.8.refs_9_.refs_14_ = bf16[512,512]{1,0:T(8,128)(2,1)} collective-permute-done((bf16[512,512]{1,0:T(8,128)(2,1)}, bf16[512,512]{1,0:T(8,128)(2,1)}, u32[]{:S(2)}, u32[]{:S(2)}) %collective-permute-start.8) | collective-permute-done | bytes 524320 | tf_op jit(solution)/shard_map/ppermute | solution.py:368
  67.9 2.1 convert_element_type.99.refs_4_
  73.1 23.6 %forward_0.1 = (bf16[4,512,128]{2,1,0:T(8,128)(2,1)}, f32[4,16,512]{2,1,0:T(8,128)}, bf16[512,512]{1,0:T(8,128)(2,1)}, f32[512,512]{1,0:T(8,128)}, f32[512,1]{1,...) custom-call(f32[1]{0:T(128)} %bitcast.1.refs_0_.bias, ...), custom_call_target="tpu_custom_call" | custom-call | flops 5000000000 | bytes 10000000 | tf_op jit(solution)/shard_map/forward_0/pallas_call | solution.py:338
  98.3 5.0 %collective-permute-done.15.refs_6_.refs_11_ = bf16[128,512]{1,0:T(8,128)(2,1)S(1)} collective-permute-done((bf16[128,512]{1,0:T(8,128)(2,1)S(1)}, bf16[128,512]{1,0:T(8,128)(2,1)S(1)}, u32[]{:S(2)}, u32[]{:S(2)}) %collective-permute-start.15) | collective-permute-done | bytes 131104 | tf_op jit(solution)/shard_map/ppermute | solution.py:368
  106.0 20.7 %forward_1.1 = (bf16[4,512,128]{2,1,0:T(8,128)(2,1)}, f32[4,16,512]{2,1,0:T(8,128)}, bf16[512,512]{1,0:T(8,128)(2,1)}, f32[512,512]{1,0:T(8,128)}, f32[512,1]{1,...) custom-call(f32[1]{0:T(128)} %bitcast.1.refs_0_.bias, ...), custom_call_target="tpu_custom_call" | custom-call | flops 5000000000 | bytes 10000000 | tf_op jit(solution)/shard_map/forward_1/pallas_call | solution.py:338
  127.6 18.6 %block_1.1 = (bf16[2,1152,512]{2,1,0:T(8,128)(2,1)}, bf16[2,1152,512]{2,1,0:T(8,128)(2,1)}, f32[512,512]{1,0:T(8,128)}, bf16[4,512,128]{2,1,0:T(8,128)(2,1)}, f3...) custom-call(bf16[512,512]{1,0:T(8,128)(2,1)} %copy-done.25, f32[512,512]{1,0:T(8,128)} %get-tuple-element.77.refs_1_, ...), custom_call_target="tpu_custom_call" | custom-call | flops 5000000000 | bytes 10000000 | tf_op jit(solution)/shard_map/block_1/pallas_call | solution.py:338
  146.2 15.9 %attention_1.1 = (bf16[4,512,128]{2,1,0:T(8,128)(2,1)}, f32[4,512,256]{2,1,0:T(8,128)}, bf16[4,512,256]{2,1,0:T(8,128)(2,1)}) custom-call(f32[1]{0:T(128)} %bitcast.1.refs_0_.bias, bf16[4,512,128]{2,1,0:T(8,128)(2,1)} %get-tuple-element.73.refs_1_.query, bf16[4,512,256]{2,1,0:T(8,128)(2,1)} %get-tuple-element.74.refs_2_.pair, ...), custom_call_target="tpu_custom_call" | custom-call | flops 5000000000 | bytes 10000000 | tf_op jit(solution)/shard_map/attention_1/pallas_call | solution.py:338
  163.5 2.5 collective-permute-done.23.away
  167.0 8.7 %input_1.1 = (bf16[2,512,384]{2,1,0:T(8,128)(2,1)}, bf16[2,512,384]{2,1,0:T(8,128)(2,1)}, f32[512,512]{1,0:T(8,128)}, f32[4,8,384]{2,1,0:T(8,128)}) custom-call(bf16[4,512,128]{2,1,0:T(8,128)(2,1)} %get-tuple-element.88.query_grad, f32[4,512,256]{2,1,0:T(8,128)} %get-tuple-element.89.here, bf16[4,512,256]{2,1,0:T(8,128)(2,1)} %copy-done.19, ...), custom_call_target="tpu_custom_call" | custom-call | flops 2000000000 | bytes 10000000 | tf_op jit(solution)/shard_map/input_1/pallas_call | solution.py:338
  176.2 18.9 %block_0.1 = (bf16[2,1152,512]{2,1,0:T(8,128)(2,1)}, bf16[2,1152,512]{2,1,0:T(8,128)(2,1)}, f32[512,512]{1,0:T(8,128)}, bf16[4,512,128]{2,1,0:T(8,128)(2,1)}, f3...) custom-call(f32[512,512]{1,0:T(8,128)} %get-tuple-element.93.refs_0_, ...), custom_call_target="tpu_custom_call" | custom-call | flops 5000000000 | bytes 10000000 | tf_op jit(solution)/shard_map/block_0/pallas_call | solution.py:338
  197.2 16.0 %attention_0.1 = (bf16[4,512,128]{2,1,0:T(8,128)(2,1)}, f32[4,512,256]{2,1,0:T(8,128)}, bf16[4,512,256]{2,1,0:T(8,128)(2,1)}) custom-call(f32[1]{0:T(128)} %bitcast.1.refs_0_.bias, bf16[4,512,128]{2,1,0:T(8,128)(2,1)} %get-tuple-element.71.refs_1_.query, bf16[4,512,256]{2,1,0:T(8,128)(2,1)} %get-tuple-element.72.refs_2_.pair, ...), custom_call_target="tpu_custom_call" | custom-call | flops 5000000000 | bytes 10000000 | tf_op jit(solution)/shard_map/attention_0/pallas_call | solution.py:338
  214.1 2.3 add_convert_fusion
  218.1 2.3 add_convert_fusion.1
  222.5 22.9 %collective-permute-done.32 = bf16[1152,512]{1,0:T(8,128)(2,1)S(1)} collective-permute-done((bf16[1152,512]{1,0:T(8,128)(2,1)S(1)}, bf16[1152,512]{1,0:T(8,128)(2,1)S(1)}, u32[]{:S(2)}, u32[]{:S(2)}) %collective-permute-start.32) | collective-permute-done | bytes 1179680 | tf_op jit(solution)/shard_map/ppermute | solution.py:368
  247.6 8.7 %input_0.1 = (bf16[2,512,384]{2,1,0:T(8,128)(2,1)}, bf16[2,512,384]{2,1,0:T(8,128)(2,1)}, f32[512,512]{1,0:T(8,128)}, f32[4,8,384]{2,1,0:T(8,128)}) custom-call(bf16[4,512,128]{2,1,0:T(8,128)(2,1)} %get-tuple-element.105.query_grad, f32[4,512,256]{2,1,0:T(8,128)} %get-tuple-element.106.here, bf16[4,512,256]{2,1,0:T(8,128)(2,1)} %collective-permute-done.24.away, ...), custom_call_target="tpu_custom_call" | custom-call | flops 2000000000 | bytes 10000000 | tf_op jit(solution)/shard_map/input_0/pallas_call | solution.py:338
  264.3 6.0 %collective-permute-done.27 = bf16[1152,512]{1,0:T(8,128)(2,1)} collective-permute-done((bf16[1152,512]{1,0:T(8,128)(2,1)S(1)}, bf16[1152,512]{1,0:T(8,128)(2,1)}, u32[]{:S(2)}, u32[]{:S(2)}) %collective-permute-start.27) | collective-permute-done | bytes 1179680 | tf_op jit(solution)/shard_map/ppermute | solution.py:368
  270.3 2.0 fusion.2.refs_0_
  272.3 64.3 %all-reduce.5.cloned.1.call-done = (bf16[512,384]{1,0:T(8,128)(2,1)}, bf16[1152,512]{1,0:T(8,128)(2,1)}) async-done(((bf16[512,384]{1,0:T(8,128)(2,1)}, bf16[1152,512]{1,0:T(8,128)(2,1)}), (bf16[512,384]{1,0:T(8,128)(2,1)}, bf16[1152,512]{1,0:T(8,128)(2,1)})) %all-reduce.5.cloned.1.call-update) | async-done | bytes 1572880 | tf_op jit(solution)/shard_map/psum | solution.py:504
  337.8 65.1 %finish.1 = (bf16[2,1152,512]{2,1,0:T(8,128)(2,1)S(1)}, bf16[2,512,384]{2,1,0:T(8,128)(2,1)S(1)}, f32[2,16,512]{2,1,0:T(8,128)S(1)}) custom-call(bf16[1152,512]{1,0:T(8,128)(2,1)S(1)} %fusion.2.refs_0_, bf16[2,512,384]{2,1,0:T(8,128)(2,1)S(1)} %copy-done, bf16[2,512,384]{2,1,0:T(8,128)(2,1)S(1)} %copy-done.1, f32[4,16,512]{2,1,0:T(8,128)S(1)} %concatenate.9.refs_3_), custom_call_target="tpu_custom_call" | custom-call | flops 1000000000 | bytes 10000000 | tf_op jit(solution)/shard_map/finish/pallas_call | solution.py:689
  405.5 2.8 convert_element_type.118
  420.5 2.4 copy.107
  422.8 2.8 fusion
  425.7 2.7 fusion.5
  429.0 3.0 copy.102
  432.1 4.0 pad_maximum_fusion
  436.1 5.5 %copy.108 = f32[2,512,1024]{2,1,0:T(8,128)} copy(f32[2,512,1024]{1,2,0:T(8,128)} %pad_maximum_fusion) | data formatting | bytes 8388608
  441.6 4.1 pad_maximum_fusion.1
  (214 shorter events, 78.0 us)
Async XLA Ops:
  7.2 329.5 %all-reduce.5.cloned.1.call-start = ((), (), s32[]{:S(2)}) async-start(), calls=%async_computation | async-start | bytes 3145728 | tf_op jit(solution)/shard_map/psum | solution.py:504
  8.5 45.7 %collective-permute-start = (f32[8,128]{1,0:T(8,128)}, f32[8,128]{1,0:T(8,128)}, u32[]{:S(2)}, u32[]{:S(2)}) collective-permute-start(f32[8,128]{1,0:T(8,128)} %broadcast_in_dim.11), channel_id=1, source_target_pairs={{0,0},{1,2},{2,1},{3,3},{4,4},{5,6},{6,5},{7,7},{8,8},{9,10},{10,9... | collective-permute-start | bytes 12296 | tf_op jit(solution)/shard_map/ppermute | solution.py:368
  11.1 28.0 %collective-permute-start.4 = (f32[2,1536]{1,0:T(2,128)S(1)}, f32[2,1536]{1,0:T(2,128)}, u32[]{:S(2)}, u32[]{:S(2)}) collective-permute-start(f32[2,1536]{1,0:T(2,128)S(1)} %pad_maximum_fusion.3), channel_id=1, source_target_pairs={{0,1},{1,0},{2,3},{3,2},{4,5},{5,4},{6,7},{7,6},{8,9},{9,8},{10,11... | collective-permute-start | bytes 36872 | tf_op jit(solution)/shard_map/ppermute | solution.py:368
  14.1 28.8 %collective-permute-start.1 = (bf16[512,512]{1,0:T(8,128)(2,1)}, bf16[512,512]{1,0:T(8,128)(2,1)}, u32[]{:S(2)}, u32[]{:S(2)}) collective-permute-start(bf16[512,512]{1,0:T(8,128)(2,1)} %param.17), channel_id=1, source_target_pairs={{0,0},{1,2},{2,1},{3,3},{4,4},{5,6},{6,5},{7,7},{8,8},{9,10},{10,9... | collective-permute-start | bytes 1572872 | tf_op jit(solution)/shard_map/ppermute | solution.py:368
  21.7 18.9 %collective-permute-start.2 = (bf16[512,384]{1,0:T(8,128)(2,1)S(1)}, bf16[512,384]{1,0:T(8,128)(2,1)}, u32[]{:S(2)}, u32[]{:S(2)}) collective-permute-start(bf16[512,384]{1,0:T(8,128)(2,1)S(1)} %bitcast.151), channel_id=1, source_target_pairs={{0,1},{1,0},{2,3},{3,2},{4,5},{5,4},{6,7},{7,6},{8,9},{9,8},{10,11... | collective-permute-start | bytes 1179656 | tf_op jit(solution)/shard_map/ppermute | solution.py:368
  22.7 42.8 %collective-permute-start.12 = (bf16[512,384]{1,0:T(8,128)(2,1)}, bf16[512,384]{1,0:T(8,128)(2,1)}, u32[]{:S(2)}, u32[]{:S(2)}) collective-permute-start(bf16[512,384]{1,0:T(8,128)(2,1)} %bitcast.23), channel_id=1, source_target_pairs={{0,1},{1,0},{2,3},{3,2},{4,5},{5,4},{6,7},{7,6},{8,9},{9,8},{10,11... | collective-permute-start | bytes 1179656 | tf_op jit(solution)/shard_map/ppermute | solution.py:368
  39.1 18.5 %collective-permute-start.10 = (bf16[512,512]{1,0:T(8,128)(2,1)}, bf16[512,512]{1,0:T(8,128)(2,1)}, u32[]{:S(2)}, u32[]{:S(2)}) collective-permute-start(bf16[512,512]{1,0:T(8,128)(2,1)} %dynamic-slice_bitcast_fusion.2), channel_id=1, source_target_pairs={{0,1},{1,0},{2,3},{3,2},{4,5},{5,4},{6,7},{7,6},{8,9},{9,8},{10,11... | collective-permute-start | bytes 1572872 | tf_op jit(solution)/shard_map/ppermute | solution.py:368
  42.9 22.7 %collective-permute-start.8 = (bf16[512,512]{1,0:T(8,128)(2,1)}, bf16[512,512]{1,0:T(8,128)(2,1)}, u32[]{:S(2)}, u32[]{:S(2)}) collective-permute-start(bf16[512,512]{1,0:T(8,128)(2,1)} %dynamic-slice_bitcast_fusion.3), channel_id=1, source_target_pairs={{0,1},{1,0},{2,3},{3,2},{4,5},{5,4},{6,7},{7,6},{8,9},{9,8},{10,11... | collective-permute-start | bytes 1572872 | tf_op jit(solution)/shard_map/ppermute | solution.py:368
  50.1 22.0 %collective-permute-start.5 = (bf16[4,512,256]{2,1,0:T(8,128)(2,1)}, bf16[4,512,256]{2,1,0:T(8,128)(2,1)}, u32[]{:S(2)}, u32[]{:S(2)}) collective-permute-start(bf16[4,512,256]{2,1,0:T(8,128)(2,1)} %get-tuple-element.72.refs_2_.pair), channel_id=1, source_target_pairs={{0,2},{1,3},{2,0},{3,1},{4,6},{5,7},{6,4},{7,5},{8,10},{9,11},{10,... | collective-permute-start | bytes 3145736 | tf_op jit(solution)/shard_map/ppermute | solution.py:368
  54.2 13.1 %collective-permute-start.6 = (bf16[128,512]{1,0:T(8,128)(2,1)S(1)}, bf16[128,512]{1,0:T(8,128)(2,1)S(1)}, u32[]{:S(2)}, u32[]{:S(2)}) collective-permute-start(bf16[128,512]{1,0:T(8,128)(2,1)S(1)} %dynamic-slice_bitcast_fusion.5), channel_id=1, source_target_pairs={{0,1},{1,0},{2,3},{3,2},{4,5},{5,4},{6,7},{7,6},{8,9},{9,8},{10,11... | collective-permute-start | bytes 393224 | tf_op jit(solution)/shard_map/ppermute | solution.py:368
  57.6 14.6 %collective-permute-start.11 = (bf16[512,512]{1,0:T(8,128)(2,1)}, bf16[512,512]{1,0:T(8,128)(2,1)S(1)}, u32[]{:S(2)}, u32[]{:S(2)}) collective-permute-start(bf16[512,512]{1,0:T(8,128)(2,1)} %collective-permute-done.10.refs_12_.refs_17_), channel_id=1, source_target_pairs={{0,2},{1,3},{2,0},{3,1},{4,6},{5,7},{6,4},{7,5},{8,10},{9,11},{10,... | collective-permute-start | bytes 1572872 | tf_op jit(solution)/shard_map/ppermute | solution.py:368
  65.5 6.6 %collective-permute-start.9 = (bf16[512,512]{1,0:T(8,128)(2,1)}, bf16[512,512]{1,0:T(8,128)(2,1)S(1)}, u32[]{:S(2)}, u32[]{:S(2)}) collective-permute-start(bf16[512,512]{1,0:T(8,128)(2,1)} %collective-permute-done.8.refs_9_.refs_14_), channel_id=1, source_target_pairs={{0,2},{1,3},{2,0},{3,1},{4,6},{5,7},{6,4},{7,5},{8,10},{9,11},{10,... | collective-permute-start | bytes 1572872 | tf_op jit(solution)/shard_map/ppermute | solution.py:368
  65.5 5.4 %collective-permute-start.13 = (bf16[512,384]{1,0:T(8,128)(2,1)}, bf16[512,384]{1,0:T(8,128)(2,1)S(1)}, u32[]{:S(2)}, u32[]{:S(2)}) collective-permute-start(bf16[512,384]{1,0:T(8,128)(2,1)} %collective-permute-done.12.refs_17_.wi_mine), channel_id=1, source_target_pairs={{0,2},{1,3},{2,0},{3,1},{4,6},{5,7},{6,4},{7,5},{8,10},{9,11},{10,... | collective-permute-start | bytes 1179656 | tf_op jit(solution)/shard_map/ppermute | solution.py:368
  70.0 26.8 %collective-permute-start.19 = (bf16[512,512]{1,0:T(8,128)(2,1)S(1)}, bf16[512,512]{1,0:T(8,128)(2,1)}, u32[]{:S(2)}, u32[]{:S(2)}) collective-permute-start(bf16[512,512]{1,0:T(8,128)(2,1)S(1)} %copy-done.12), channel_id=1, source_target_pairs={{0,1},{1,0},{2,3},{3,2},{4,5},{5,4},{6,7},{7,6},{8,9},{9,8},{10,11... | collective-permute-start | bytes 1572872 | tf_op jit(solution)/shard_map/ppermute | solution.py:368
  70.9 26.4 %collective-permute-start.17 = (bf16[512,512]{1,0:T(8,128)(2,1)S(1)}, bf16[512,512]{1,0:T(8,128)(2,1)}, u32[]{:S(2)}, u32[]{:S(2)}) collective-permute-start(bf16[512,512]{1,0:T(8,128)(2,1)S(1)} %dynamic-slice_bitcast_fusion.1), channel_id=1, source_target_pairs={{0,1},{1,0},{2,3},{3,2},{4,5},{5,4},{6,7},{7,6},{8,9},{9,8},{10,11... | collective-permute-start | bytes 1572872 | tf_op jit(solution)/shard_map/ppermute | solution.py:368
  96.8 8.0 %collective-permute-start.14 = (bf16[4,512,256]{2,1,0:T(8,128)(2,1)}, bf16[4,512,256]{2,1,0:T(8,128)(2,1)S(1)}, u32[]{:S(2)}, u32[]{:S(2)}) collective-permute-start(bf16[4,512,256]{2,1,0:T(8,128)(2,1)} %get-tuple-element.74.refs_2_.pair), channel_id=1, source_target_pairs={{0,2},{1,3},{2,0},{3,1},{4,6},{5,7},{6,4},{7,5},{8,10},{9,11},{10,... | collective-permute-start | bytes 3145736 | tf_op jit(solution)/shard_map/ppermute | solution.py:368
  96.8 7.8 %collective-permute-start.20 = (bf16[512,512]{1,0:T(8,128)(2,1)}, bf16[512,512]{1,0:T(8,128)(2,1)S(1)}, u32[]{:S(2)}, u32[]{:S(2)}) collective-permute-start(bf16[512,512]{1,0:T(8,128)(2,1)} %collective-permute-done.19.refs_12_.refs_17_), channel_id=1, source_target_pairs={{0,2},{1,3},{2,0},{3,1},{4,6},{5,7},{6,4},{7,5},{8,10},{9,11},{10,... | collective-permute-start | bytes 1572872 | tf_op jit(solution)/shard_map/ppermute | solution.py:368
  97.3 7.4 %collective-permute-start.18 = (bf16[512,512]{1,0:T(8,128)(2,1)}, bf16[512,512]{1,0:T(8,128)(2,1)S(1)}, u32[]{:S(2)}, u32[]{:S(2)}) collective-permute-start(bf16[512,512]{1,0:T(8,128)(2,1)} %collective-permute-done.17.refs_9_.refs_14_), channel_id=1, source_target_pairs={{0,2},{1,3},{2,0},{3,1},{4,6},{5,7},{6,4},{7,5},{8,10},{9,11},{10,... | collective-permute-start | bytes 1572872 | tf_op jit(solution)/shard_map/ppermute | solution.py:368
  97.4 5.9 %collective-permute-start.15 = (bf16[128,512]{1,0:T(8,128)(2,1)S(1)}, bf16[128,512]{1,0:T(8,128)(2,1)S(1)}, u32[]{:S(2)}, u32[]{:S(2)}) collective-permute-start(bf16[128,512]{1,0:T(8,128)(2,1)S(1)} %dynamic-slice_bitcast_fusion.4), channel_id=1, source_target_pairs={{0,1},{1,0},{2,3},{3,2},{4,5},{5,4},{6,7},{7,6},{8,9},{9,8},{10,11... | collective-permute-start | bytes 393224 | tf_op jit(solution)/shard_map/ppermute | solution.py:368
  103.3 23.5 %collective-permute-start.22 = (bf16[512,512]{1,0:T(8,128)(2,1)S(1)}, bf16[512,512]{1,0:T(8,128)(2,1)S(1)}, u32[]{:S(2)}, u32[]{:S(2)}) collective-permute-start(bf16[512,512]{1,0:T(8,128)(2,1)S(1)} %copy-done.20), channel_id=1, source_target_pairs={{0,0},{1,2},{2,1},{3,3},{4,4},{5,6},{6,5},{7,7},{8,8},{9,10},{10,9... | collective-permute-start | bytes 1572872 | tf_op jit(solution)/shard_map/ppermute | solution.py:368
  162.0 4.0 collective-permute-start.23
  163.5 50.6 %collective-permute-start.31 = (bf16[2,1152,512]{2,1,0:T(8,128)(2,1)}, bf16[2,1152,512]{2,1,0:T(8,128)(2,1)}, u32[]{:S(2)}, u32[]{:S(2)}) collective-permute-start(bf16[2,1152,512]{2,1,0:T(8,128)(2,1)} %get-tuple-element.126), channel_id=1, source_target_pairs={{0,2},{1,3},{2,0},{3,1},{4,6},{5,7},{6,4},{7,5},{8,10},{9,11},{10,... | collective-permute-start | bytes 7077896 | tf_op jit(solution)/shard_map/ppermute | solution.py:368
  175.7 19.6 %collective-permute-start.28 = (bf16[2,512,384]{2,1,0:T(8,128)(2,1)}, bf16[2,512,384]{2,1,0:T(8,128)(2,1)S(1)}, u32[]{:S(2)}, u32[]{:S(2)}) collective-permute-start(bf16[2,512,384]{2,1,0:T(8,128)(2,1)} %get-tuple-element.122), channel_id=1, source_target_pairs={{0,2},{1,3},{2,0},{3,1},{4,6},{5,7},{6,4},{7,5},{8,10},{9,11},{10,... | collective-permute-start | bytes 2359304 | tf_op jit(solution)/shard_map/ppermute | solution.py:368
  195.1 22.0 %collective-permute-start.26 = (bf16[2,1152,512]{2,1,0:T(8,128)(2,1)}, bf16[2,1152,512]{2,1,0:T(8,128)(2,1)}, u32[]{:S(2)}, u32[]{:S(2)}) collective-permute-start(bf16[2,1152,512]{2,1,0:T(8,128)(2,1)} %get-tuple-element.111), channel_id=1, source_target_pairs={{0,2},{1,3},{2,0},{3,1},{4,6},{5,7},{6,4},{7,5},{8,10},{9,11},{10,... | collective-permute-start | bytes 7077896 | tf_op jit(solution)/shard_map/ppermute | solution.py:368
  195.6 17.7 %collective-permute-start.29 = (bf16[512,384]{1,0:T(8,128)(2,1)S(1)}, bf16[512,384]{1,0:T(8,128)(2,1)S(1)}, u32[]{:S(2)}, u32[]{:S(2)}) collective-permute-start(bf16[512,384]{1,0:T(8,128)(2,1)S(1)} %slice_bitcast_fusion.6), channel_id=1, source_target_pairs={{0,1},{1,0},{2,3},{3,2},{4,5},{5,4},{6,7},{7,6},{8,9},{9,8},{10,11... | collective-permute-start | bytes 1179656 | tf_op jit(solution)/shard_map/ppermute | solution.py:368
  213.2 34.4 %collective-permute-start.24 = (bf16[4,512,256]{2,1,0:T(8,128)(2,1)}, bf16[4,512,256]{2,1,0:T(8,128)(2,1)}, u32[]{:S(2)}, u32[]{:S(2)}) collective-permute-start(bf16[4,512,256]{2,1,0:T(8,128)(2,1)} %get-tuple-element.107), channel_id=1, source_target_pairs={{0,2},{1,3},{2,0},{3,1},{4,6},{5,7},{6,4},{7,5},{8,10},{9,11},{10,... | collective-permute-start | bytes 3145736 | tf_op jit(solution)/shard_map/ppermute | solution.py:368
  216.5 28.9 %collective-permute-start.32 = (bf16[1152,512]{1,0:T(8,128)(2,1)S(1)}, bf16[1152,512]{1,0:T(8,128)(2,1)S(1)}, u32[]{:S(2)}, u32[]{:S(2)}) collective-permute-start(bf16[1152,512]{1,0:T(8,128)(2,1)S(1)} %slice_bitcast_fusion.2), channel_id=1, source_target_pairs={{0,1},{1,0},{2,3},{3,2},{4,5},{5,4},{6,7},{7,6},{8,9},{9,8},{10,11... | collective-permute-start | bytes 3538952 | tf_op jit(solution)/shard_map/ppermute | solution.py:368
  221.9 48.4 %collective-permute-start.27 = (bf16[1152,512]{1,0:T(8,128)(2,1)S(1)}, bf16[1152,512]{1,0:T(8,128)(2,1)}, u32[]{:S(2)}, u32[]{:S(2)}) collective-permute-start(bf16[1152,512]{1,0:T(8,128)(2,1)S(1)} %slice_bitcast_fusion.4), channel_id=1, source_target_pairs={{0,1},{1,0},{2,3},{3,2},{4,5},{5,4},{6,7},{7,6},{8,9},{9,8},{10,11... | collective-permute-start | bytes 3538952 | tf_op jit(solution)/shard_map/ppermute | solution.py:368
  246.9 12.6 %collective-permute-start.21 = (bf16[512,512]{1,0:T(8,128)(2,1)S(1)}, bf16[512,512]{1,0:T(8,128)(2,1)S(1)}, u32[]{:S(2)}, u32[]{:S(2)}) collective-permute-start(bf16[512,512]{1,0:T(8,128)(2,1)S(1)} %convert_element_type.100), channel_id=1, source_target_pairs={{0,0},{1,2},{2,1},{3,3},{4,4},{5,6},{6,5},{7,7},{8,8},{9,10},{10,9... | collective-permute-start | bytes 1572872 | tf_op jit(solution)/shard_map/ppermute | solution.py:368
  257.7 5.5 %collective-permute-start.25 = (bf16[512,512]{1,0:T(8,128)(2,1)S(1)}, bf16[512,512]{1,0:T(8,128)(2,1)S(1)}, u32[]{:S(2)}, u32[]{:S(2)}) collective-permute-start(bf16[512,512]{1,0:T(8,128)(2,1)S(1)} %convert_element_type.102), channel_id=1, source_target_pairs={{0,0},{1,2},{2,1},{3,3},{4,4},{5,6},{6,5},{7,7},{8,8},{9,10},{10,9... | collective-permute-start | bytes 1572872 | tf_op jit(solution)/shard_map/ppermute | solution.py:368
  336.6 86.2 %collective-permute-start.33 = (bf16[1152,512]{1,0:T(8,128)(2,1)}, bf16[1152,512]{1,0:T(8,128)(2,1)}, u32[]{:S(2)}, u32[]{:S(2)}) collective-permute-start(bf16[1152,512]{1,0:T(8,128)(2,1)} %get-tuple-element.158), channel_id=1, source_target_pairs={{0,2},{1,3},{2,0},{3,1},{4,6},{5,7},{6,4},{7,5},{8,10},{9,11},{10,... | collective-permute-start | bytes 3538952 | tf_op jit(solution)/shard_map/ppermute | solution.py:368
  413.8 4.9 %collective-permute-start.30 = (bf16[512,384]{1,0:T(8,128)(2,1)S(1)}, bf16[512,384]{1,0:T(8,128)(2,1)S(1)}, u32[]{:S(2)}, u32[]{:S(2)}) collective-permute-start(bf16[512,384]{1,0:T(8,128)(2,1)S(1)} %copy-done.13), channel_id=1, source_target_pairs={{0,2},{1,3},{2,0},{3,1},{4,6},{5,7},{6,4},{7,5},{8,10},{9,11},{10,... | collective-permute-start | bytes 1179656 | tf_op jit(solution)/shard_map/ppermute | solution.py:368
  (36 other events, 265.2 us)
Sparse Core Ops, SparseCore 0:
  246.9 89.6 all-reduce.4
